TPU v7x, 256 devices: a whole 4x4x8 slice. The times are simulated.
256 devices in a mesh: dp: 32 (over x, z_lo, y), tensor: 8 (over z_hi, core).
Axes of the slice: x: 4, y: 4, z: 8 (z_hi: 4, z_lo: 2; z = z_hi * 2 + z_lo), core: 2. Of those that a mesh axis runs over, the one named last changes fastest.
Arguments:
- gradient: bfloat16 [2, 2048, 16384], P(None, 'dp', 'tensor'), may hold values from -1000 to 1000
- master: float32 [2, 2048, 16384], P(None, 'dp', 'tensor'), may hold values from -0.046875 to 0.046875
- first_moment: float32 [2, 2048, 16384], P(None, 'dp', 'tensor'), may hold values from -3 to 3
- second_moment: float32 [2, 2048, 16384], P(None, 'dp', 'tensor'), may hold values from 0.05 to 1
- residual: bfloat16 [8192, 16384], P('dp', 'tensor'), may hold values from -1500 to 1500
- norm_gain: float32 [16384], replicated, may hold values from 0.5 to 2
- queries: bfloat16 [8192, 128, 128], P('dp', 'tensor'), may hold values from -170 to 170
- layer_cache: bfloat16 [8192, 2, 8, 32, 128], P('dp', None, 'tensor'), may hold values from -4.5 to 4.5
- fresh_entries: bfloat16 [8192, 2, 8, 128], P('dp', None, 'tensor'), may hold values from -6 to 6
- lengths: int32 [8192], P('dp'), may hold values from 2 to 32, as said below
- shard_table: int32 [32], replicated, may hold values from 0 to 31, each once
Outputs:
- new_first: float32 [2, 2048, 16384], P(None, 'dp', 'tensor')
- new_second: float32 [2, 2048, 16384], P(None, 'dp', 'tensor')
- attended: bfloat16 [8192, 128, 128], P('dp', 'tensor')
- activated: bfloat16 [8192, 2048], P('dp', 'tensor')
Inputs may be any that keep to these rules, and one draw needn't show every extreme that they name: `lengths`: every row has 2 or more valid positions, and in each rollout group's rows one row has all 32. `shard_table`: A permutation of the learner shards.
All inputs are finite; a program needn't handle non-finite values.
Results may differ from a plain program's by a relative error of at most 0.0072.
Values may be sent and summed in bfloat16 or wider, within the bound.
A program may use at most 128 MiB of HBM per device.

v0:
```python
import math

import jax
import jax.numpy as jnp
from jax import lax
from jax.sharding import PartitionSpec as P

LEARN_RATE = 0.001
CLIP_LEVEL = 0.5
CLIP_EPSILON = 1e-06
FIRST_DECAY = 0.9
SECOND_DECAY = 0.95
FIRST_CORRECTION = 1.0 - 0.9**10
SECOND_CORRECTION = 1.0 - 0.95**10
ADAM_EPSILON = 1e-08
NORM_EPSILON = 1e-05


def adam_update(gradient, master, first_moment, second_moment):
    entry_count = (
        gradient.shape[0]
        * gradient.shape[1]
        * lax.axis_size("dp")
        * gradient.shape[2]
        * lax.axis_size("tensor")
    )
    gradient_wide = gradient.astype(jnp.float32)
    local_sum = jnp.sum(gradient_wide * gradient_wide)
    total_sum = lax.psum(local_sum, ("dp", "tensor"))
    clip_limit = CLIP_LEVEL * math.sqrt(entry_count)
    clip_factor = jnp.minimum(1.0, clip_limit / (jnp.sqrt(total_sum) + CLIP_EPSILON))
    clipped = gradient_wide * clip_factor
    new_first = FIRST_DECAY * first_moment + (1.0 - FIRST_DECAY) * clipped
    new_second = SECOND_DECAY * second_moment + (1.0 - SECOND_DECAY) * clipped * clipped
    adam_step = (
        new_first / FIRST_CORRECTION / (jnp.sqrt(new_second / SECOND_CORRECTION) + ADAM_EPSILON)
    )
    fresh_weight = (master - LEARN_RATE * adam_step).astype(jnp.bfloat16)
    return (new_first, new_second, fresh_weight)


def attend(queries, layer_cache, fresh_entries, lengths):
    row_count, head_count, head_width = queries.shape
    group_count = layer_cache.shape[2]
    per_group = head_count // group_count
    score_scale = 1.0 / math.sqrt(head_width)
    grouped = queries.reshape(row_count, group_count, per_group, head_width)
    cached_keys = layer_cache[:, 0]
    cached_values = layer_cache[:, 1]
    scores = (
        jnp.einsum("rghd,rgpd->rghp", grouped, cached_keys, preferred_element_type=jnp.float32)
        * score_scale
    )
    own_score = (
        jnp.einsum(
            "rghd,rgd->rgh", grouped, fresh_entries[:, 0], preferred_element_type=jnp.float32
        )
        * score_scale
    )
    positions = lax.broadcasted_iota(jnp.int32, (row_count, 1, 1, cached_keys.shape[2]), 3)
    in_range = positions < lengths[:, None, None, None]
    scores = jnp.where(in_range, scores, -jnp.inf)
    row_peak = jnp.maximum(jnp.max(scores, axis=3), own_score)
    cached_exp = jnp.exp(scores - row_peak[..., None])
    own_exp = jnp.exp(own_score - row_peak)
    denominator = jnp.sum(cached_exp, axis=3) + own_exp
    cached_prob = (cached_exp / denominator[..., None]).astype(jnp.bfloat16)
    own_prob = (own_exp / denominator).astype(jnp.bfloat16)
    combined = jnp.einsum(
        "rghp,rgpd->rghd", cached_prob, cached_values, preferred_element_type=jnp.float32
    )
    combined = (
        combined
        + own_prob[..., None].astype(jnp.float32)
        * fresh_entries[:, 1].astype(jnp.float32)[:, :, None, :]
    )
    return combined.reshape(row_count, head_count, head_width).astype(jnp.bfloat16)


def per_device(
    gradient,
    master,
    first_moment,
    second_moment,
    residual,
    norm_gain,
    queries,
    layer_cache,
    fresh_entries,
    lengths,
    shard_table,
):
    new_first, new_second, fresh_weight = adam_update(gradient, master, first_moment, second_moment)
    row_count = residual.shape[0]
    shard_count = lax.axis_size("dp")
    rank_count = lax.axis_size("tensor")
    unit_block = fresh_weight.shape[1] // rank_count
    gathered = lax.all_gather(residual, "tensor", axis=1, tiled=True)
    gathered_wide = gathered.astype(jnp.float32)
    mean_square = jnp.mean(gathered_wide * gathered_wide, axis=1, keepdims=True)
    normed = (gathered_wide * lax.rsqrt(mean_square + NORM_EPSILON) * norm_gain).astype(
        jnp.bfloat16
    )
    regrouped = lax.all_to_all(fresh_weight, "tensor", split_axis=1, concat_axis=2, tiled=True)
    projected = jnp.einsum(
        "xk,cuk->xcu",
        normed,
        lax.all_gather(regrouped, "dp", axis=1, tiled=True),
        preferred_element_type=jnp.float32,
    )
    projected = projected.reshape(row_count, 2, shard_count, unit_block)
    hidden = jax.nn.silu(projected[:, 0]) * projected[:, 1]
    ordered = jnp.take(hidden, shard_table, axis=1)
    activated = ordered.reshape(row_count, shard_count * unit_block).astype(jnp.bfloat16)
    attended = attend(queries, layer_cache, fresh_entries, lengths)
    return (new_first, new_second, attended, activated)


def solution(mesh):
    return jax.shard_map(
        per_device,
        mesh=mesh,
        in_specs=(
            P(None, "dp", "tensor"),
            P(None, "dp", "tensor"),
            P(None, "dp", "tensor"),
            P(None, "dp", "tensor"),
            P("dp", "tensor"),
            P(),
            P("dp", "tensor", None),
            P("dp", None, "tensor", None, None),
            P("dp", None, "tensor", None),
            P("dp"),
            P(),
        ),
        out_specs=(
            P(None, "dp", "tensor"),
            P(None, "dp", "tensor"),
            P("dp", "tensor", None),
            P("dp", "tensor"),
        ),
        check_vma=False,
    )
```

profile of v0, /device:TPU:1, one launch (start us, length us, event | category | flops | bytes accessed | tf_op | source)
XLA Modules:
  0.0 355.7 jit_solution(8791076577248445641)
XLA Ops:
  7.2 0.7 all-gather.3.cloned.1.call-update
  7.9 0.0 all-gather.5.cloned.1.call-start
  8.0 1.9 fusion.23
  9.9 113.1 %psum.7 = f32[]{:T(128)} all-reduce(f32[]{:T(128)} %fusion.23), channel_id=1, replica_groups=mesh['dp'=32,'tensor'=8] {'dp','tensor'}, use_global_device_ids=true, to_apply=%region_1.0 | all-reduce | flops 1 | bytes 8 | tf_op jit(solution)/shard_map/psum | solution.py:29
  123.7 3.8 %subtract_convert_fusion = (bf16[2,64,2048]{2,1,0:T(8,128)(2,1)S(1)}, f32[2,64,2048]{2,1,0:T(8,128)}, f32[2,64,2048]{2,1,0:T(8,128)}) fusion(f32[2,64,2048]{2,1,0:T(8,128)S(1)} %copy-done.1, f32[]{:T(128)S(6)} %min_shard_map.3, bf16[2,64,2048]{2,1,0:T(8,128)(2,1)} %param.11, f32[2,64,2048]{2,1,0:T(8,128)} %param.14, f32[2,64,2048]{2,1,0:T(8,128)} %param.13), kind=kLoop, calls=%fused_computation.30 | loop fusion | flops 4194304 | bytes 6291460 | tf_op jit(solution)/shard_map/convert_element_type | solution.py:38
  127.5 0.5 copy.36
  128.1 21.6 %all_to_all.18 = bf16[2,64,2048]{2,0,1:T(2,128)(2,1)S(1)} all-to-all(bf16[2,64,2048]{2,0,1:T(2,128)(2,1)S(1)} %copy.36), channel_id=1, replica_groups=mesh['dp'=32,'tensor'=8] {'tensor'}, dimensions={1} | all-to-all | bytes 1048576 | tf_op jit(solution)/shard_map/all_to_all | solution.py:104
  149.7 1.0 copy.37
  150.8 0.2 fusion.40
  151.0 0.1 broadcast_in_dim.37
  151.1 0.1 broadcast_in_dim.38
  151.2 0.1 iota_compare_fusion
  151.3 0.7 fusion.32
  152.0 3.1 fusion.14
  155.1 1.3 fusion.15
  156.4 0.1 fusion.35
  156.5 3.7 %add_convert_fusion = bf16[256,16,128]{2,1,0:T(8,128)(2,1)} fusion(bf16[256,2,1,32,128]{4,3,2,1,0:T(8,128)(2,1)S(1)} %copy-done.2, f32[256,16,32]{2,1,0:T(8,128)S(1)} %get-tuple-element.24, f32[256,128]{1,0:T(8,128)S(1)} %bitcast.54, f32[256,16]{1,0:T(8,128)S(1)} %get-tuple-element.20, f32[256,16]{1,0:T(8,128)S(1)} %get-tuple-element.19, ...), kind=kOutput, calls=%fused_computation.14 | convolution fusion | flops 35782656 | bytes 5799936 | tf_op jit(solution)/shard_map/rghp,rgpd->rghd/dot_general | solution.py:69
  160.2 5.2 %fusion = f32[256]{0:T(256)S(1)} fusion(bf16[256,16384]{1,0:T(8,128)(2,1)} %all-gather.3.cloned.1.call-done), kind=kLoop, calls=%fused_computation.3 | loop fusion | flops 12582656 | bytes 8389632 | tf_op jit(solution)/shard_map/reduce_sum | solution.py:100
  165.4 170.0 %all-gather.5.cloned.1.call-done = bf16[2,256,16384]{2,1,0:T(8,128)(2,1)} async-done(((bf16[2,8,16384]{2,1,0:T(8,128)(2,1)}), bf16[2,256,16384]{2,1,0:T(8,128)(2,1)}) %all-gather.5.cloned.1.call-update) | async-done | bytes 16777232 | tf_op jit(solution)/shard_map/all_gather | solution.py:108
  335.3 12.0 %fusion.19 = f32[256,2,32,8]{0,3,2,1:T(8,128)S(1)} fusion(bf16[2,256,16384]{2,1,0:T(8,128)(2,1)} %all-gather.5.cloned.1.call-done, bf16[256,16384]{1,0:T(8,128)(2,1)} %all-gather.3.cloned.1.call-done, f32[16384]{0:T(1024)S(1)} %copy-done.5, f32[256]{0:T(256)S(1)} %add_rsqrt_fusion), kind=kOutput, calls=%fused_computation.26 | convolution fusion | flops 4311744512 | bytes 25756672 | tf_op jit(solution)/shard_map/xk,cuk->xcu/dot_general | solution.py:105
  347.4 0.1 fusion.30
  347.4 0.6 gather_fusion
  348.0 0.1 fusion.31
  348.1 0.8 copy.38
  (23 shorter events, 0.1 us)
Async XLA Ops:
  7.2 144.1 %copy-start = (bf16[256,16,128]{2,1,0:T(8,128)(2,1)S(1)}, bf16[256,16,128]{2,1,0:T(8,128)(2,1)}, u32[]{:S(2)}) copy-start(bf16[256,16,128]{2,1,0:T(8,128)(2,1)} %param.17) | copy-start | bytes 3145732
  7.2 116.5 %copy-start.1 = (f32[2,64,2048]{2,1,0:T(8,128)S(1)}, f32[2,64,2048]{2,1,0:T(8,128)}, u32[]{:S(2)}) copy-start(f32[2,64,2048]{2,1,0:T(8,128)} %param.12) | copy-start | bytes 3145732
  7.2 153.0 %all-gather.3.cloned.1.call-start = ((), (), s32[]{:S(2)}) async-start(), calls=%async_computation.1 | async-start | bytes 9437184 | tf_op jit(solution)/shard_map/all_gather | solution.py:98
  7.9 327.4 %all-gather.5.cloned.1.call-start = ((), (), s32[]{:S(2)}) async-start(), calls=%async_computation.2 | async-start | bytes 17301504 | tf_op jit(solution)/shard_map/all_gather | solution.py:108
  127.5 23.2 %copy-start.3 = (bf16[256,2,1,128]{3,1,2,0:T(2,128)(2,1)S(1)}, bf16[256,2,1,128]{3,1,2,0:T(2,128)(2,1)}, u32[]{:S(2)}) copy-start(bf16[256,2,1,128]{3,1,2,0:T(2,128)(2,1)} %param.19) | copy-start | bytes 393220
  127.5 23.4 %copy-start.6 = (s32[32]{0:T(128)S(1)}, s32[32]{0:T(128)}, u32[]{:S(2)}) copy-start(s32[32]{0:T(128)} %param.21) | copy-start | bytes 388
  127.5 23.7 %copy-start.4 = (s32[256]{0:T(256)S(1)}, s32[256]{0:T(256)}, u32[]{:S(2)}) copy-start(s32[256]{0:T(256)} %param.20) | copy-start | bytes 3076
  152.0 4.5 %copy-start.2 = (bf16[256,2,1,32,128]{4,3,2,1,0:T(8,128)(2,1)S(1)}, bf16[256,2,1,32,128]{4,3,2,1,0:T(8,128)(2,1)}, u32[]{:S(2)}) copy-start(bf16[256,2,1,32,128]{4,3,2,1,0:T(8,128)(2,1)} %param.18) | copy-start | bytes 12582916
  160.2 175.1 %copy-start.5 = (f32[16384]{0:T(1024)S(1)}, f32[16384]{0:T(1024)}, u32[]{:S(2)}) copy-start(f32[16384]{0:T(1024)} %param.16) | copy-start | bytes 196612
Sparse Core Ops, SparseCore 0:
  9.9 92.9 all-gather.2
  150.9 184.4 all-gather.4
where the time goes:
time: 360 us; the launch traced here: 356 us
  waiting for transfers between devices  171 us (48%)
  blocking collectives  135 us (38%)
  matrix products  19.5 us (5%)
  between operations  15 us (4%)
  other arithmetic  12.8 us (4%)
    all_gather x1, waiting for transfers between devices, per_device(): lax.all_gather(regrouped, 'dp', axis=1, tiled=True)  170 us
    psum x1, blocking collectives, adam_update(): total_sum = lax.psum(local_sum, ('dp', 'tensor'))  113 us
    all_to_all x1, blocking collectives, per_device(): lax.all_to_all(fresh_weight, 'tensor', split_axis=1, concat_axis=2, tiled...  21.6 us
    dot_general x1, matrix products, per_device(): jnp.einsum('xk,cuk->xcu', normed, lax.all_gather(regrouped, 'dp', axis=1,...  12 us
  transfers between devices with their start and end apart: 2, of which 1 were waited for; matrix products, arithmetic and copies ran while one was open for 6% of the time, Pallas kernels for 0%

commit v1 on v0

v1 whole, which is shorter than its diff:
```python
import math

import jax
import jax.numpy as jnp
from jax import lax
from jax.experimental import pallas as pl
from jax.experimental.pallas import tpu as pltpu
from jax.sharding import PartitionSpec as P

LEARN_RATE = 0.001
CLIP_LEVEL = 0.5
CLIP_EPSILON = 1e-06
FIRST_DECAY = 0.9
SECOND_DECAY = 0.95
FIRST_CORRECTION = 1.0 - 0.9**10
SECOND_CORRECTION = 1.0 - 0.95**10
ADAM_EPSILON = 1e-08
NORM_EPSILON = 1e-05

MESH = pl.DeviceIdType.MESH
F32 = jnp.float32
BF16 = jnp.bfloat16

K_DEV = 2048
ROWS = 256
UNITS = 64
WIDTH = 16384


class Remote:
    def __init__(self, src, dst, sends, recvs, slot, device, arrives=None):
        self.copy = pltpu.make_async_remote_copy(
            src_ref=src, dst_ref=dst, send_sem=sends.at[slot], recv_sem=recvs.at[slot],
            device_id=device, device_id_type=MESH)
        arrives = dst if arrives is None else arrives
        self.inbound = pltpu.make_async_remote_copy(
            src_ref=arrives, dst_ref=arrives, send_sem=sends.at[slot], recv_sem=recvs.at[slot],
            device_id=device, device_id_type=MESH)
        self.copy.start()

    def sent(self):
        self.copy.wait_send()

    def came(self):
        self.inbound.wait_recv()


N_COPIES = 56


def step_kernel(
    clip_limit,
    grad_h, master_h, first_h, second_h, resid_h, gain_h, table_ref,
    act_ref, clip_ref,
    g_v, ma_v, m_v, v_v, gf, gain_v, a_v, b_v, b_swap, c_s, c_r, h_s, h_r,
    p_s, p_r, t_s, t_r, s_g, load_sem, sends, recvs, many,
):
    d = lax.axis_index("dp")
    t = lax.axis_index("tensor")
    x, zl, y = d // 8, (d // 4) % 2, d % 4
    zh, c = t // 2, t % 2
    oc = 1 - c
    xp, xq = x + 1 - 2 * (x % 2), (x + 3 + 2 * (x % 2)) % 4
    yp, yq = y + 1 - 2 * (y % 2), (y + 3 + 2 * (y % 2)) % 4

    def at(x_, zl_, y_, zh_=None, c_=None):
        zh_ = zh if zh_ is None else zh_
        c_ = c if c_ is None else c_
        return {"dp": x_ * 8 + zl_ * 4 + y_, "tensor": zh_ * 2 + c_}

    to_xp, to_yp, to_diag = at(xp, zl, y), at(x, zl, yp), at(xp, zl, yp)
    to_xq, to_yq, to_zl = at(xq, zl, y), at(x, zl, yq), at(x, 1 - zl, y)
    to_core = at(x, zl, y, zh, oc)

    barrier = pltpu.get_barrier_semaphore()
    for k in range(1, 8):
        pl.semaphore_signal(barrier, inc=1, device_id={"dp": d, "tensor": (t + k) % 8}, device_id_type=MESH)
    for k in range(1, 32):
        pl.semaphore_signal(barrier, inc=1, device_id={"dp": (d + k) % 32, "tensor": t}, device_id_type=MESH)

    loads = [
        pltpu.make_async_copy(grad_h, g_v, load_sem.at[0]),
        pltpu.make_async_copy(resid_h, a_v.at[0, c], load_sem.at[1]),
        pltpu.make_async_copy(gain_h.at[pl.ds(pl.multiple_of(t * 16, 16), 16)], gain_v, load_sem.at[2]),
        pltpu.make_async_copy(master_h, ma_v, load_sem.at[3]),
        pltpu.make_async_copy(first_h, m_v, load_sem.at[4]),
        pltpu.make_async_copy(second_h, v_v, load_sem.at[5]),
    ]
    for load in loads:
        load.start()

    used = []

    def remote(src, dst, device, arrives=None):
        r = Remote(src, dst, sends, recvs, len(used), device, arrives)
        used.append(r)
        return r

    loads[0].wait()

    def square(i, acc):
        g = g_v[i // 4, pl.ds(pl.multiple_of((i % 4) * 16, 16), 16), :].astype(F32)
        gf[i // 4, pl.ds(pl.multiple_of((i % 4) * 16, 16), 16), :] = g
        sq = g * g
        return acc + (sq[:8] + sq[8:])

    acc = lax.fori_loop(0, 8, square, jnp.zeros((8, K_DEV), F32))
    local = jnp.sum(jnp.sum(acc, axis=0, keepdims=True), axis=1, keepdims=True)
    p_s[...] = jnp.broadcast_to(local, (8, 128))

    pl.semaphore_wait(barrier, 38)

    for k in range(1, 32):
        pltpu.make_async_remote_copy(
            src_ref=p_s, dst_ref=p_r.at[k - 1], send_sem=many.at[0], recv_sem=many.at[1],
            device_id={"dp": (d + k) % 32, "tensor": t}, device_id_type=MESH).start()

    loads[1].wait()
    ones = jnp.ones((8, 512), BF16)
    row_squares = jnp.zeros((8, ROWS), F32)
    for k in range(4):
        r = a_v[0, c, :, k * 512:(k + 1) * 512].astype(F32)
        sq = r * r
        high = sq.astype(BF16)
        low = (sq - high.astype(F32)).astype(BF16)
        for part in (high, low):
            row_squares += lax.dot_general(ones, part, (((1,), (1,)), ((), ())), preferred_element_type=F32)

    everyone = pltpu.make_async_remote_copy(
        src_ref=p_r, dst_ref=p_r, send_sem=many.at[0], recv_sem=many.at[1],
        device_id=to_core, device_id_type=MESH)
    everyone.wait_send()
    everyone.wait_recv()
    total = p_s[...]
    for k in range(31):
        total += p_r[k]
    t_s[:, :128] = total
    t_s[:, 128:] = row_squares

    for k in range(1, 8):
        pltpu.make_async_remote_copy(
            src_ref=t_s, dst_ref=t_r.at[k - 1], send_sem=many.at[2], recv_sem=many.at[3],
            device_id={"dp": d, "tensor": (t + k) % 8}, device_id_type=MESH).start()

    def rows_of(slot, half, r):
        return a_v.at[slot, half, pl.ds(r * 128, 128)]

    def to_other_core(slot, r):
        return remote(rows_of(slot, c, r), rows_of(slot, c, r), to_core, rows_of(slot, oc, r))

    rows_x = [remote(rows_of(0, c, r), rows_of(1, c, r), to_xp) for r in range(2)]
    rows_y = [remote(rows_of(0, c, r), rows_of(2, c, r), to_yp) for r in range(2)]
    core_rows = [to_other_core(0, 0), to_other_core(0, 1)]

    team = pltpu.make_async_remote_copy(
        src_ref=t_r, dst_ref=t_r, send_sem=many.at[2], recv_sem=many.at[3],
        device_id=to_core, device_id_type=MESH)
    team.wait_send()
    team.wait_recv()
    both = t_s[...]
    for k in range(7):
        both += t_r[k]
    clip = jnp.minimum(1.0, clip_limit / (jnp.sqrt(both[:, :128]) + CLIP_EPSILON))
    clip_ref[...] = clip
    s_g[0] = both[:, 128:]
    square_copies = [remote(s_g.at[0], s_g.at[slot], device) for slot, device in ((1, to_xp), (2, to_yp), (3, to_diag))]

    for load in loads[2:]:
        load.wait()
    clip_one = clip[0:1, 0:1]
    gain = jnp.concatenate([gain_v[i:i + 1, :] for i in range(16)], axis=1)

    def fresh(parity, zone):
        row = pl.multiple_of((2 * zone + parity) * 8, 8)
        parts = []
        for i in range(2):
            clipped = gf[i, pl.ds(row, 8), :] * clip_one
            new_first = FIRST_DECAY * m_v[i, pl.ds(row, 8), :] + (1.0 - FIRST_DECAY) * clipped
            new_second = SECOND_DECAY * v_v[i, pl.ds(row, 8), :] + (1.0 - SECOND_DECAY) * clipped * clipped
            step = (new_first * (LEARN_RATE / FIRST_CORRECTION)) / (
                jnp.sqrt(new_second * (1.0 / SECOND_CORRECTION)) + ADAM_EPSILON)
            parts.append((ma_v[i, pl.ds(row, 8), :] - step) * gain)
        return jnp.concatenate(parts, axis=0).astype(BF16)

    @pl.loop(0, 4)
    def _(zone):
        b_swap[pl.ds(pl.multiple_of(zone * 16, 16), 16), :] = fresh(oc, zone)

    swap = remote(b_swap, b_v.at[0, c], to_core, b_v.at[0, oc])

    @pl.loop(0, 4)
    def _(zone):
        b_v[0, c, pl.ds(pl.multiple_of(zone * 16, 16), 16), :] = fresh(c, zone)

    def piece(slot, k):
        return b_v.at[slot, c if k == 0 else oc]

    def units(src, dst, k, device):
        return remote(piece(src, k), piece(dst, k), device)

    unit = {}
    for k in range(2):
        if k == 1:
            swap.came()
        unit[1, k] = units(0, 1, k, to_zl)
        unit[2, k] = units(0, 2, k, to_xq)
        unit[4, k] = units(0, 4, k, to_yq)

    core_got = []
    diag = []

    def pass_rows(r):
        rows_x[r].came()
        core_got.append(to_other_core(1, r))
        if r == 0:
            diag.append(remote(rows_of(1, c, 0), rows_of(3, c, 0), to_yp))
        rows_y[r].came()
        core_got.append(to_other_core(2, r))
        if r == 1:
            diag.append(remote(rows_of(2, c, 1), rows_of(3, c, 1), to_xp))

    pass_rows(0)
    for k in range(2):
        unit[1, k].came()
        unit[3, k] = units(1, 3, k, to_xq)
        unit[5, k] = units(1, 5, k, to_yq)
    unit[2, 0].came()
    unit[6, 0] = units(2, 6, 0, to_yq)
    unit[4, 0].came()
    unit[4, 1].came()
    unit[6, 1] = units(4, 6, 1, to_xq)
    unit[2, 1].came()
    pass_rows(1)
    for r in core_rows + core_got:
        r.came()

    def product(slot, count, a):
        out = jnp.zeros((count * UNITS, ROWS), F32)
        for h in range(2):
            lhs = b_v[slot:slot + count, h].reshape(count * UNITS, K_DEV)
            out += lax.dot_general(lhs, a_v[a, h], (((1,), (1,)), ((), ())), preferred_element_type=F32)
        return out.reshape(count, 4, 16, ROWS).astype(BF16)

    def pair_tile(p, a):
        out = product(2 * p, 2, a)
        for z in range(4):
            c_s[p, z, a] = out[:, z]

    sums = []

    def send_sums(view_s, view_r):
        for k in range(1, 4):
            z = (zh + k) % 4
            sums.append(remote(view_s(z), view_r(k - 1), at(x, zl, y, z, c)))

    def pair_three(p):
        @pl.loop(0, 3)
        def _(a):
            pair_tile(p, a)

        send_sums(lambda z: c_s.at[p, z, pl.ds(0, 3)], lambda k: c_r.at[k, p, pl.ds(0, 3)])

    pair_three(0)
    unit[3, 0].came()
    unit[7, 0] = units(3, 7, 0, to_yq)
    unit[5, 0].came()
    unit[5, 1].came()
    unit[7, 1] = units(5, 7, 1, to_xq)
    unit[3, 1].came()
    pair_three(1)
    pair_three(2)
    last_rows = []
    for r in range(2):
        diag[r].came()
        last_rows.append(to_other_core(3, r))
    for r in last_rows:
        r.came()
    for p in range(3):
        pair_tile(p, 3)
    send_sums(lambda z: c_s.at[pl.ds(0, 3), z, 3], lambda k: c_r.at[k, pl.ds(0, 3), 3])

    for q in range(2):
        for k in range(2):
            unit[6 + q, k].came()

        @pl.loop(0, 4)
        def _(a):
            out = product(6 + q, 1, a)
            for z in range(4):
                c_s[3, z, a, q] = out[0, z]

        send_sums(lambda z: c_s.at[3, z, :, q], lambda k: c_r.at[k, 3, :, q])

    for r in square_copies:
        r.came()
    for r in sums:
        r.came()
    outs = []
    for a, device in ((1, to_xp), (2, to_yp), (3, to_diag), (0, None)):
        scale = lax.rsqrt(s_g[a][0:1, :] * (1.0 / WIDTH) + NORM_EPSILON)
        for p in range(4):
            v = c_s[p, zh, a].astype(F32)
            for k in range(3):
                v += c_r[k, p, a].astype(F32)
            gate = v[:, :8] * scale
            up = v[:, 8:] * scale
            hidden = (gate / (1.0 + jnp.exp(-gate)) * up).reshape(16, ROWS).astype(BF16)
            if device is None:
                h_r[0, p * 16:(p + 1) * 16, :] = hidden
            else:
                h_s[a - 1, p * 16:(p + 1) * 16, :] = hidden
        if device is not None:
            outs.append(remote(h_s.at[a - 1], h_r.at[a], device))

    u = lax.broadcasted_iota(jnp.int32, (256, 256), 0)
    col = lax.broadcasted_iota(jnp.int32, (256, 256), 1)
    slot, pair, zbit = u // 64, (u // 16) % 4, (u // 8) % 2
    xs = jnp.where(slot % 2 == 1, xp, x)
    ys = jnp.where(slot // 2 == 1, yp, y)
    xs = jnp.where(pair % 2 == 1, (xs + 3 + 2 * (xs % 2)) % 4, xs)
    ys = jnp.where(pair // 2 == 1, (ys + 3 + 2 * (ys % 2)) % 4, ys)
    zs = jnp.where(zbit == 1, 1 - zl, zl)
    shard = xs * 8 + zs * 4 + ys
    spread = (lax.broadcasted_iota(jnp.int32, (32, 256), 0)
              == lax.broadcasted_iota(jnp.int32, (32, 256), 1) // 8).astype(F32).astype(BF16)
    table = jnp.broadcast_to(table_ref[...].astype(F32), (8, 32)).astype(BF16)
    wanted = jnp.dot(table, spread, preferred_element_type=F32)[0:1, :].astype(jnp.int32)
    pick = jnp.where((shard == wanted) & (u % 8 == col % 8), 1.0, 0.0).astype(BF16)
    for r in outs:
        r.came()
    act_ref[...] = lax.dot_general(
        h_r[...].reshape(256, ROWS), pick, (((0,), (0,)), ((), ())), preferred_element_type=F32).astype(BF16)

    for r in used:
        r.sent()
    assert len(used) <= N_COPIES, len(used)


def gather_and_project(gradient, master, first_moment, second_moment, residual, norm_gain, shard_table, clip_limit):
    hbm = pl.BlockSpec(memory_space=pl.ANY)
    vmem = pl.BlockSpec(memory_space=pltpu.VMEM)
    slab = gradient.shape

    def kernel(*refs):
        step_kernel(clip_limit, *refs)

    return pl.pallas_call(
        kernel,
        out_shape=(
            jax.ShapeDtypeStruct((ROWS, 256), BF16),
            jax.ShapeDtypeStruct((8, 128), F32),
        ),
        in_specs=[hbm] * 6 + [vmem],
        out_specs=(vmem, vmem),
        scratch_shapes=[
            pltpu.VMEM(slab, BF16),
            pltpu.VMEM(slab, F32),
            pltpu.VMEM(slab, F32),
            pltpu.VMEM(slab, F32),
            pltpu.VMEM(slab, F32),
            pltpu.VMEM((16, 128), F32),
            pltpu.VMEM((4, 2, ROWS, K_DEV), BF16),
            pltpu.VMEM((8, 2, UNITS, K_DEV), BF16),
            pltpu.VMEM((UNITS, K_DEV), BF16),
            pltpu.VMEM((4, 4, 4, 2, 16, ROWS), BF16),
            pltpu.VMEM((3, 4, 4, 2, 16, ROWS), BF16),
            pltpu.VMEM((3, UNITS, ROWS), BF16),
            pltpu.VMEM((4, UNITS, ROWS), BF16),
            pltpu.VMEM((8, 128), F32),
            pltpu.VMEM((31, 8, 128), F32),
            pltpu.VMEM((8, 384), F32),
            pltpu.VMEM((7, 8, 384), F32),
            pltpu.VMEM((4, 8, ROWS), F32),
            pltpu.SemaphoreType.DMA((6,)),
            pltpu.SemaphoreType.DMA((N_COPIES,)),
            pltpu.SemaphoreType.DMA((N_COPIES,)),
            pltpu.SemaphoreType.DMA((4,)),
        ],
        compiler_params=pltpu.CompilerParams(
            collective_id=0, has_side_effects=True, vmem_limit_bytes=48 << 20),
        cost_estimate=pl.CostEstimate(
            flops=2 * 512 * 1024 * 4096, bytes_accessed=8 << 20, transcendentals=1 << 20),
        name="gather_project",
    )(gradient, master, first_moment, second_moment, residual,
      norm_gain.reshape(128, 128), shard_table.reshape(1, 32))


def attend(queries, layer_cache, fresh_entries, lengths):
    row_count, head_count, head_width = queries.shape
    group_count = layer_cache.shape[2]
    per_group = head_count // group_count
    score_scale = 1.0 / math.sqrt(head_width)
    grouped = queries.reshape(row_count, group_count, per_group, head_width)
    cached_keys = layer_cache[:, 0]
    cached_values = layer_cache[:, 1]
    scores = (
        jnp.einsum("rghd,rgpd->rghp", grouped, cached_keys, preferred_element_type=jnp.float32)
        * score_scale
    )
    own_score = (
        jnp.einsum(
            "rghd,rgd->rgh", grouped, fresh_entries[:, 0], preferred_element_type=jnp.float32
        )
        * score_scale
    )
    positions = lax.broadcasted_iota(jnp.int32, (row_count, 1, 1, cached_keys.shape[2]), 3)
    in_range = positions < lengths[:, None, None, None]
    scores = jnp.where(in_range, scores, -jnp.inf)
    row_peak = jnp.maximum(jnp.max(scores, axis=3), own_score)
    cached_exp = jnp.exp(scores - row_peak[..., None])
    own_exp = jnp.exp(own_score - row_peak)
    denominator = jnp.sum(cached_exp, axis=3) + own_exp
    cached_prob = (cached_exp / denominator[..., None]).astype(jnp.bfloat16)
    own_prob = (own_exp / denominator).astype(jnp.bfloat16)
    combined = jnp.einsum(
        "rghp,rgpd->rghd", cached_prob, cached_values, preferred_element_type=jnp.float32
    )
    combined = (
        combined
        + own_prob[..., None].astype(jnp.float32)
        * fresh_entries[:, 1].astype(jnp.float32)[:, :, None, :]
    )
    return combined.reshape(row_count, head_count, head_width).astype(jnp.bfloat16)


def per_device(
    gradient,
    master,
    first_moment,
    second_moment,
    residual,
    norm_gain,
    queries,
    layer_cache,
    fresh_entries,
    lengths,
    shard_table,
):
    entry_count = gradient.size * lax.axis_size("dp") * lax.axis_size("tensor")
    activated, clip = gather_and_project(
        gradient, master, first_moment, second_moment, residual, norm_gain, shard_table,
        CLIP_LEVEL * math.sqrt(entry_count))
    clipped = gradient.astype(jnp.float32) * clip[0, 0]
    new_first = FIRST_DECAY * first_moment + (1.0 - FIRST_DECAY) * clipped
    new_second = SECOND_DECAY * second_moment + (1.0 - SECOND_DECAY) * clipped * clipped
    attended = attend(queries, layer_cache, fresh_entries, lengths)
    return (new_first, new_second, attended, activated)


def solution(mesh):
    return jax.shard_map(
        per_device,
        mesh=mesh,
        in_specs=(
            P(None, "dp", "tensor"),
            P(None, "dp", "tensor"),
            P(None, "dp", "tensor"),
            P(None, "dp", "tensor"),
            P("dp", "tensor"),
            P(),
            P("dp", "tensor", None),
            P("dp", None, "tensor", None, None),
            P("dp", None, "tensor", None),
            P("dp"),
            P(),
        ),
        out_specs=(
            P(None, "dp", "tensor"),
            P(None, "dp", "tensor"),
            P("dp", "tensor", None),
            P("dp", "tensor"),
        ),
        check_vma=False,
    )
```

time: 360 us -> 90 us (0.25); the launches traced: 356 us -> 89.9 us
  waiting for transfers between devices: 171 us -> 0 us
  blocking collectives: 135 us -> 0 us
  Pallas kernels: 0 us -> 75.3 us
  between operations: 15 us -> 0.78 us
  matrix products: 19.5 us -> 7.31 us
  other arithmetic: 12.8 us -> 4.79 us
    all_gather x2 -> x0, waiting for transfers between devices: 170 us -> none  [the longest x1 170 us: per_device(): lax.all_gather(regrouped, 'dp', axis=1, tiled=True)]
    psum x1 -> x0, blocking collectives: 113 us -> none  [adam_update(): total_sum = lax.psum(local_sum, ('dp', 'tensor'))]
    pallas_call x0 -> x1, Pallas kernels: none -> 75.3 us  [gather_and_project(): pl.pallas_call(kernel, out_shape=(jax.ShapeDtypeStruct((ROWS, 256), BF16)...]
    all_to_all x1 -> x0, blocking collectives: 21.6 us -> none  [per_device(): lax.all_to_all(fresh_weight, 'tensor', split_axis=1, concat_axis=2, tiled...]
    dot_general x1 -> x0, matrix products: 12 us -> none  [per_device(): jnp.einsum('xk,cuk->xcu', normed, lax.all_gather(regrouped, 'dp', axis=1,...]
    reduce_sum x2 -> x0, other arithmetic: 7.09 us -> none  [the longest x1 5.17 us: per_device(): mean_square = jnp.mean(gathered_wide * gathered_wide, axis=1, keepdims=True)]
    convert_element_type x2 -> x0, other arithmetic: 3.91 us -> none  [the longest x1 3.8 us: adam_update(): fresh_weight = (master - LEARN_RATE * adam_step).astype(jnp.bfloat16)]
  transfers between devices with their start and end apart: 2 -> 0, of which waited for: 1 -> 0; matrix products, arithmetic and copies ran while one was open for 6% -> 0% of each run, Pallas kernels for 0% -> 0%
where the time goes in v1:
time: 90 us; the launch traced here: 89.9 us
  Pallas kernels  75.3 us (84%)
  matrix products  7.31 us (8%)
  other arithmetic  4.79 us (5%)
  local copies, waits for them, and re-layouts  1.72 us (2%)
    pallas_call x1, Pallas kernels, gather_and_project(): pl.pallas_call(kernel, out_shape=(jax.ShapeDtypeStruct((ROWS, 256), BF16)...  75.3 us
    dot_general x1, matrix products, attend(): jnp.einsum('rghp,rgpd->rghd', cached_prob, cached_values, preferred_eleme...  3.71 us
    dot_general x1, matrix products, attend(): jnp.einsum('rghd,rgpd->rghp', grouped, cached_keys, preferred_element_typ...  2.95 us
    add x1, other arithmetic, per_device(): SECOND_DECAY * second_moment + (1.0 - SECOND_DECAY) * clipped * clipped  2.37 us

profile of v1, /device:TPU:1, one launch (start us, length us, event | category | flops | bytes accessed | tf_op | source)
XLA Modules:
  0.0 89.9 jit_solution(14606187400192519716)
XLA Ops:
  0.6 0.0 copy-start
  0.6 0.9 iota_compare_fusion
  1.5 0.4 copy-done
  1.9 2.9 %fusion.6 = (f32[256,16]{1,0:T(8,128)S(1)}, f32[256,16,32]{2,1,0:T(8,128)S(1)}) fusion(pred[256,32]{1,0:T(8,128)(4,1)S(1)} %iota_compare_fusion, bf16[256,16,128]{2,1,0:T(8,128)(2,1)S(1)} %copy-done, bf16[256,2,1,32,128]{4,3,2,1,0:T(8,128)(2,1)} %param.18), kind=kOutput, calls=%fused_computation.10 | convolution fusion | flops 33943552 | bytes 3694592 | tf_op jit(solution)/shard_map/rghd,rgpd->rghp/dot_general | solution.py:397
  4.8 0.0 copy-done.9
  4.8 0.2 fusion.22
  5.1 0.0 copy-start.8
  5.1 0.7 fusion.16
  5.8 1.3 %fusion.7 = f32[256,16]{1,0:T(8,128)S(1)} fusion(f32[256,16,32]{2,1,0:T(8,128)S(1)} %get-tuple-element.15, f32[256,16]{1,0:T(8,128)S(1)} %multiply_maximum_fusion, pred[256,32]{1,0:T(8,128)(4,1)S(1)} %iota_compare_fusion), kind=kLoop, calls=%fused_computation.11 | loop fusion | flops 520192 | bytes 565248 | tf_op jit(solution)/shard_map/reduce_sum | solution.py:412
  7.1 0.1 fusion.19
  7.1 0.1 copy-done.8
  7.3 0.0 copy-start.5
  7.3 0.0 copy-start.6
  7.3 0.0 copy-start.7
  7.3 3.7 %add_convert_fusion = bf16[256,16,128]{2,1,0:T(8,128)(2,1)} fusion(bf16[256,2,1,32,128]{4,3,2,1,0:T(8,128)(2,1)S(1)} %copy-done.8, f32[256,16,32]{2,1,0:T(8,128)S(1)} %get-tuple-element.15, f32[256,128]{1,0:T(8,128)S(1)} %bitcast.31, f32[256,16]{1,0:T(8,128)S(1)} %get-tuple-element.11, f32[256,16]{1,0:T(8,128)S(1)} %get-tuple-element.10, ...), kind=kOutput, calls=%fused_computation.4 | convolution fusion | flops 35782656 | bytes 5799936 | tf_op jit(solution)/shard_map/rghp,rgpd->rghd/dot_general | solution.py:415
  11.0 0.0 copy-done.1
  11.0 0.0 copy-done.2
  11.0 0.0 copy-done.3
  11.0 0.0 copy-done.4
  11.0 0.0 copy-done.5
  11.1 75.3 %gather_project.1 = (bf16[256,256]{1,0:T(8,128)(2,1)S(1)}, f32[8,128]{1,0:T(8,128)S(1)}) custom-call(bf16[2,64,2048]{2,1,0:T(8,128)(2,1)S(1)} %copy-done.3, f32[2,64,2048]{2,1,0:T(8,128)S(1)} %copy-done.4, f32[2,64,2048]{2,1,0:T(8,128)S(1)} %copy-done.2, f32[2,64,2048]{2,1,0:T(8,128)S(1)} %copy-done.1, bf16[256,2048]{1,0:T(8,128)(2,1)S(1)} %copy-done.5, ...), custom_call_target="tpu_custom_call" | custom-call | flops 4294967296 | bytes 8388608 | tf_op jit(solution)/shard_map/gather_project/pallas_call | solution.py:347
  86.3 0.5 slice.15
  86.8 2.4 %fusion.10 = (f32[2,64,2048]{2,1,0:T(8,128)}, f32[2,64,2048]{2,1,0:T(8,128)}) fusion(f32[2,64,2048]{2,1,0:T(8,128)S(1)} %copy-done.1, bf16[2,64,2048]{2,1,0:T(8,128)(2,1)S(1)} %copy-done.3, f32[]{:T(128)} %bitcast.2, f32[2,64,2048]{2,1,0:T(8,128)S(1)} %copy-done.2), kind=kLoop, calls=%fused_computation.13 | loop fusion | flops 2359296 | bytes 4718596 | tf_op jit(solution)/shard_map/add | solution.py:445
  89.2 0.7 copy.30
  (9 shorter events, 0.0 us)
Async XLA Ops:
  0.6 1.2 %copy-start = (bf16[256,16,128]{2,1,0:T(8,128)(2,1)S(1)}, bf16[256,16,128]{2,1,0:T(8,128)(2,1)}, u32[]{:S(2)}) copy-start(bf16[256,16,128]{2,1,0:T(8,128)(2,1)} %param.17) | copy-start | bytes 3145732
  1.9 3.0 %copy-start.9 = (bf16[256,2,1,128]{3,1,2,0:T(2,128)(2,1)S(1)}, bf16[256,2,1,128]{3,1,2,0:T(2,128)(2,1)}, u32[]{:S(2)}) copy-start(bf16[256,2,1,128]{3,1,2,0:T(2,128)(2,1)} %param.19) | copy-start | bytes 393220
  5.1 2.2 %copy-start.8 = (bf16[256,2,1,32,128]{4,3,2,1,0:T(8,128)(2,1)S(1)}, bf16[256,2,1,32,128]{4,3,2,1,0:T(8,128)(2,1)}, u32[]{:S(2)}) copy-start(bf16[256,2,1,32,128]{4,3,2,1,0:T(8,128)(2,1)} %param.18) | copy-start | bytes 12582916
  7.2 3.8 %copy-start.1 = (f32[2,64,2048]{2,1,0:T(8,128)S(1)}, f32[2,64,2048]{2,1,0:T(8,128)}, u32[]{:S(2)}) copy-start(f32[2,64,2048]{2,1,0:T(8,128)} %refs_3_.1) | copy-start | bytes 3145732
  7.2 3.8 %copy-start.2 = (f32[2,64,2048]{2,1,0:T(8,128)S(1)}, f32[2,64,2048]{2,1,0:T(8,128)}, u32[]{:S(2)}) copy-start(f32[2,64,2048]{2,1,0:T(8,128)} %refs_2_.1) | copy-start | bytes 3145732
  7.3 3.8 %copy-start.3 = (bf16[2,64,2048]{2,1,0:T(8,128)(2,1)S(1)}, bf16[2,64,2048]{2,1,0:T(8,128)(2,1)}, u32[]{:S(2)}) copy-start(bf16[2,64,2048]{2,1,0:T(8,128)(2,1)} %refs_0_.1) | copy-start | bytes 1572868
  7.3 3.8 %copy-start.4 = (f32[2,64,2048]{2,1,0:T(8,128)S(1)}, f32[2,64,2048]{2,1,0:T(8,128)}, u32[]{:S(2)}) copy-start(f32[2,64,2048]{2,1,0:T(8,128)} %refs_1_.1) | copy-start | bytes 3145732
  7.3 3.8 %copy-start.5 = (bf16[256,2048]{1,0:T(8,128)(2,1)S(1)}, bf16[256,2048]{1,0:T(8,128)(2,1)}, u32[]{:S(2)}) copy-start(bf16[256,2048]{1,0:T(8,128)(2,1)} %refs_4_.1) | copy-start | bytes 3145732
  7.3 3.8 %copy-start.6 = (f32[16384]{0:T(1024)S(1)}, f32[16384]{0:T(1024)}, u32[]{:S(2)}) copy-start(f32[16384]{0:T(1024)} %param.16) | copy-start | bytes 196612
  7.3 3.8 %copy-start.7 = (s32[32]{0:T(128)S(1)}, s32[32]{0:T(128)}, u32[]{:S(2)}) copy-start(s32[32]{0:T(128)} %param.21) | copy-start | bytes 388

commit v2 on v1

--- a/solution.py
+++ b/solution.py
@@ -16,6 +16,7 @@
 SECOND_CORRECTION = 1.0 - 0.95**10
 ADAM_EPSILON = 1e-08
 NORM_EPSILON = 1e-05
+SCORE_SCALE = 1.0 / math.sqrt(128)
 
 MESH = pl.DeviceIdType.MESH
 F32 = jnp.float32
@@ -50,10 +51,10 @@
 
 def step_kernel(
     clip_limit,
-    grad_h, master_h, first_h, second_h, resid_h, gain_h, table_ref,
-    act_ref, clip_ref,
+    grad_h, master_h, first_h, second_h, resid_h, gain_h, query_h, cache_h, fresh_h, length_ref, table_ref,
+    first_o, second_o, attended_o, act_ref,
     g_v, ma_v, m_v, v_v, gf, gain_v, a_v, b_v, b_swap, c_s, c_r, h_s, h_r,
-    p_s, p_r, t_s, t_r, s_g, load_sem, sends, recvs, many,
+    p_s, p_r, t_s, t_r, s_g, q_v, kv_v, f_v, o_v, len_v, load_sem, sends, recvs, many,
 ):
     d = lax.axis_index("dp")
     t = lax.axis_index("tensor")
@@ -85,6 +86,9 @@
         pltpu.make_async_copy(master_h, ma_v, load_sem.at[3]),
         pltpu.make_async_copy(first_h, m_v, load_sem.at[4]),
         pltpu.make_async_copy(second_h, v_v, load_sem.at[5]),
+        pltpu.make_async_copy(query_h, q_v, load_sem.at[6]),
+        pltpu.make_async_copy(fresh_h, f_v, load_sem.at[7]),
+        pltpu.make_async_copy(cache_h, kv_v, load_sem.at[8]),
     ]
     for load in loads:
         load.start()
@@ -126,6 +130,49 @@
         for part in (high, low):
             row_squares += lax.dot_general(ones, part, (((1,), (1,)), ((), ())), preferred_element_type=F32)
 
+    t_s[:, 128:] = row_squares
+
+    row8 = lax.broadcasted_iota(jnp.int32, (32, ROWS), 1)
+    spread_len = jnp.where(
+        lax.broadcasted_iota(jnp.int32, (ROWS, 256), 0) % 8
+        == lax.broadcasted_iota(jnp.int32, (ROWS, 256), 1) // 32, 1.0, 0.0).astype(BF16)
+    own_len = jnp.where(
+        row8 // 8 == lax.broadcasted_iota(jnp.int32, (32, ROWS), 0),
+        jnp.broadcast_to(length_ref[...].astype(F32), (32, ROWS)), 0.0).astype(BF16)
+    len_v[...] = jnp.dot(own_len, spread_len, preferred_element_type=F32)
+    for load in loads[6:]:
+        load.wait()
+
+    def attend_block(g):
+        rows = pl.ds(pl.multiple_of(g * 8, 8), 8)
+        q = q_v[rows].reshape(128, 128)
+        keys = kv_v[rows, 0].reshape(256, 128)
+        values = kv_v[rows, 1].reshape(256, 128)
+        own = f_v[rows, :]
+        own_key = jnp.broadcast_to(own[:, :128].reshape(8, 1, 128), (8, 16, 128)).reshape(128, 128)
+        own_value = jnp.broadcast_to(own[:, 128:].reshape(8, 1, 128), (8, 16, 128)).reshape(128, 128)
+        head = lax.broadcasted_iota(jnp.int32, (128, 256), 0)
+        pos = lax.broadcasted_iota(jnp.int32, (128, 256), 1)
+        scores = lax.dot_general(q, keys, (((1,), (1,)), ((), ())), preferred_element_type=F32) * SCORE_SCALE
+        own_score = jnp.sum(q.astype(F32) * own_key, axis=1, keepdims=True) * SCORE_SCALE
+        valid = (head // 16 == pos // 32) & ((pos % 32).astype(F32) < len_v[pl.ds(g, 1), :])
+        scores = jnp.where(valid, scores, -jnp.inf)
+        peak = jnp.maximum(jnp.max(scores, axis=1, keepdims=True), own_score)
+        cached = jnp.exp(scores - peak)
+        fresh_exp = jnp.exp(own_score - peak)
+        inverse = 1.0 / (jnp.sum(cached, axis=1, keepdims=True) + fresh_exp)
+        prob = (cached * inverse).astype(BF16)
+        own_prob = (fresh_exp * inverse).astype(BF16).astype(F32)
+        out = jnp.dot(prob, values, preferred_element_type=F32) + own_prob * own_value
+        o_v[rows] = out.astype(BF16).reshape(8, 16, 128)
+
+    def attend(first, last):
+        @pl.loop(first, last)
+        def _(g):
+            attend_block(g)
+
+    attend(0, 8)
+
     everyone = pltpu.make_async_remote_copy(
         src_ref=p_r, dst_ref=p_r, send_sem=many.at[0], recv_sem=many.at[1],
         device_id=to_core, device_id_type=MESH)
@@ -135,7 +182,6 @@
     for k in range(31):
         total += p_r[k]
     t_s[:, :128] = total
-    t_s[:, 128:] = row_squares
 
     for k in range(1, 8):
         pltpu.make_async_remote_copy(
@@ -151,6 +197,8 @@
     rows_x = [remote(rows_of(0, c, r), rows_of(1, c, r), to_xp) for r in range(2)]
     rows_y = [remote(rows_of(0, c, r), rows_of(2, c, r), to_yp) for r in range(2)]
     core_rows = [to_other_core(0, 0), to_other_core(0, 1)]
+
+    attend(8, 18)
 
     team = pltpu.make_async_remote_copy(
         src_ref=t_r, dst_ref=t_r, send_sem=many.at[2], recv_sem=many.at[3],
@@ -161,11 +209,10 @@
     for k in range(7):
         both += t_r[k]
     clip = jnp.minimum(1.0, clip_limit / (jnp.sqrt(both[:, :128]) + CLIP_EPSILON))
-    clip_ref[...] = clip
     s_g[0] = both[:, 128:]
     square_copies = [remote(s_g.at[0], s_g.at[slot], device) for slot, device in ((1, to_xp), (2, to_yp), (3, to_diag))]
 
-    for load in loads[2:]:
+    for load in loads[2:6]:
         load.wait()
     clip_one = clip[0:1, 0:1]
     gain = jnp.concatenate([gain_v[i:i + 1, :] for i in range(16)], axis=1)
@@ -179,6 +226,8 @@
             new_second = SECOND_DECAY * v_v[i, pl.ds(row, 8), :] + (1.0 - SECOND_DECAY) * clipped * clipped
             step = (new_first * (LEARN_RATE / FIRST_CORRECTION)) / (
                 jnp.sqrt(new_second * (1.0 / SECOND_CORRECTION)) + ADAM_EPSILON)
+            m_v[i, pl.ds(row, 8), :] = new_first
+            v_v[i, pl.ds(row, 8), :] = new_second
             parts.append((ma_v[i, pl.ds(row, 8), :] - step) * gain)
         return jnp.concatenate(parts, axis=0).astype(BF16)
 
@@ -205,6 +254,16 @@
         unit[1, k] = units(0, 1, k, to_zl)
         unit[2, k] = units(0, 2, k, to_xq)
         unit[4, k] = units(0, 4, k, to_yq)
+
+    stores = [
+        pltpu.make_async_copy(m_v, first_o, load_sem.at[9]),
+        pltpu.make_async_copy(v_v, second_o, load_sem.at[10]),
+        pltpu.make_async_copy(o_v, attended_o, load_sem.at[11]),
+    ]
+    stores[0].start()
+    stores[1].start()
+    attend(18, 32)
+    stores[2].start()
 
     core_got = []
     diag = []
@@ -331,12 +390,15 @@
     act_ref[...] = lax.dot_general(
         h_r[...].reshape(256, ROWS), pick, (((0,), (0,)), ((), ())), preferred_element_type=F32).astype(BF16)
 
+    for store in stores:
+        store.wait()
     for r in used:
         r.sent()
     assert len(used) <= N_COPIES, len(used)
 
 
-def gather_and_project(gradient, master, first_moment, second_moment, residual, norm_gain, shard_table, clip_limit):
+def step(gradient, master, first_moment, second_moment, residual, norm_gain,
+         queries, layer_cache, fresh_entries, lengths, shard_table, clip_limit):
     hbm = pl.BlockSpec(memory_space=pl.ANY)
     vmem = pl.BlockSpec(memory_space=pltpu.VMEM)
     slab = gradient.shape
@@ -347,11 +409,13 @@
     return pl.pallas_call(
         kernel,
         out_shape=(
+            jax.ShapeDtypeStruct(slab, F32),
+            jax.ShapeDtypeStruct(slab, F32),
+            jax.ShapeDtypeStruct(queries.shape, BF16),
             jax.ShapeDtypeStruct((ROWS, 256), BF16),
-            jax.ShapeDtypeStruct((8, 128), F32),
         ),
-        in_specs=[hbm] * 6 + [vmem],
-        out_specs=(vmem, vmem),
+        in_specs=[hbm] * 9 + [vmem] * 2,
+        out_specs=(hbm, hbm, hbm, vmem),
         scratch_shapes=[
             pltpu.VMEM(slab, BF16),
             pltpu.VMEM(slab, F32),
@@ -371,80 +435,31 @@
             pltpu.VMEM((8, 384), F32),
             pltpu.VMEM((7, 8, 384), F32),
             pltpu.VMEM((4, 8, ROWS), F32),
-            pltpu.SemaphoreType.DMA((6,)),
+            pltpu.VMEM(queries.shape, BF16),
+            pltpu.VMEM((ROWS, 2, 32, 128), BF16),
+            pltpu.VMEM((ROWS, 256), F32),
+            pltpu.VMEM(queries.shape, BF16),
+            pltpu.VMEM((32, 256), F32),
+            pltpu.SemaphoreType.DMA((12,)),
             pltpu.SemaphoreType.DMA((N_COPIES,)),
             pltpu.SemaphoreType.DMA((N_COPIES,)),
             pltpu.SemaphoreType.DMA((4,)),
         ],
         compiler_params=pltpu.CompilerParams(
-            collective_id=0, has_side_effects=True, vmem_limit_bytes=48 << 20),
-        cost_estimate=pl.CostEstimate(
-            flops=2 * 512 * 1024 * 4096, bytes_accessed=8 << 20, transcendentals=1 << 20),
-        name="gather_project",
+            collective_id=0, has_side_effects=True, vmem_limit_bytes=56 << 20),
+        name="step",
     )(gradient, master, first_moment, second_moment, residual,
-      norm_gain.reshape(128, 128), shard_table.reshape(1, 32))
-
-
-def attend(queries, layer_cache, fresh_entries, lengths):
-    row_count, head_count, head_width = queries.shape
-    group_count = layer_cache.shape[2]
-    per_group = head_count // group_count
-    score_scale = 1.0 / math.sqrt(head_width)
-    grouped = queries.reshape(row_count, group_count, per_group, head_width)
-    cached_keys = layer_cache[:, 0]
-    cached_values = layer_cache[:, 1]
-    scores = (
-        jnp.einsum("rghd,rgpd->rghp", grouped, cached_keys, preferred_element_type=jnp.float32)
-        * score_scale
-    )
-    own_score = (
-        jnp.einsum(
-            "rghd,rgd->rgh", grouped, fresh_entries[:, 0], preferred_element_type=jnp.float32
-        )
-        * score_scale
-    )
-    positions = lax.broadcasted_iota(jnp.int32, (row_count, 1, 1, cached_keys.shape[2]), 3)
-    in_range = positions < lengths[:, None, None, None]
-    scores = jnp.where(in_range, scores, -jnp.inf)
-    row_peak = jnp.maximum(jnp.max(scores, axis=3), own_score)
-    cached_exp = jnp.exp(scores - row_peak[..., None])
-    own_exp = jnp.exp(own_score - row_peak)
-    denominator = jnp.sum(cached_exp, axis=3) + own_exp
-    cached_prob = (cached_exp / denominator[..., None]).astype(jnp.bfloat16)
-    own_prob = (own_exp / denominator).astype(jnp.bfloat16)
-    combined = jnp.einsum(
-        "rghp,rgpd->rghd", cached_prob, cached_values, preferred_element_type=jnp.float32
-    )
-    combined = (
-        combined
-        + own_prob[..., None].astype(jnp.float32)
-        * fresh_entries[:, 1].astype(jnp.float32)[:, :, None, :]
-    )
-    return combined.reshape(row_count, head_count, head_width).astype(jnp.bfloat16)
-
-
-def per_device(
-    gradient,
-    master,
-    first_moment,
-    second_moment,
-    residual,
-    norm_gain,
-    queries,
-    layer_cache,
-    fresh_entries,
-    lengths,
-    shard_table,
-):
+      norm_gain.reshape(128, 128), queries, layer_cache.reshape(ROWS, 2, 32, 128),
+      fresh_entries.astype(F32).reshape(ROWS, 256), lengths.reshape(1, ROWS), shard_table.reshape(1, 32))
+
+
+def per_device(gradient, master, first_moment, second_moment, residual, norm_gain,
+               queries, layer_cache, fresh_entries, lengths, shard_table):
     entry_count = gradient.size * lax.axis_size("dp") * lax.axis_size("tensor")
-    activated, clip = gather_and_project(
-        gradient, master, first_moment, second_moment, residual, norm_gain, shard_table,
+    return step(
+        gradient, master, first_moment, second_moment, residual, norm_gain,
+        queries, layer_cache, fresh_entries, lengths, shard_table,
         CLIP_LEVEL * math.sqrt(entry_count))
-    clipped = gradient.astype(jnp.float32) * clip[0, 0]
-    new_first = FIRST_DECAY * first_moment + (1.0 - FIRST_DECAY) * clipped
-    new_second = SECOND_DECAY * second_moment + (1.0 - SECOND_DECAY) * clipped * clipped
-    attended = attend(queries, layer_cache, fresh_entries, lengths)
-    return (new_first, new_second, attended, activated)
 
 
 def solution(mesh):

time: 90 us -> 85.3 us (0.948)
  matrix products: 7.31 us -> 0 us
  local copies, waits for them, and re-layouts: 1.72 us -> 7.94 us
  other arithmetic: 4.79 us -> 0 us
  Pallas kernels: 75.3 us -> 76.5 us
    dot_general x3 -> x0, matrix products: 7.31 us -> none  [the longest x1 3.71 us: attend(): jnp.einsum('rghp,rgpd->rghd', cached_prob, cached_values, preferred_eleme...]
    unnamed x22 -> x9, local copies, waits for them, and re-layouts: 1.2 us -> 7.94 us
    add x2 -> x0, other arithmetic: 2.42 us -> none  [the longest x1 2.37 us: per_device(): SECOND_DECAY * second_moment + (1.0 - SECOND_DECAY) * clipped * clipped]
    reduce_sum x1 -> x0, other arithmetic: 1.3 us -> none  [attend(): denominator = jnp.sum(cached_exp, axis=3) + own_exp]
    pallas_call x1, Pallas kernels: 75.3 us -> 76.5 us  [step(): pl.pallas_call(kernel, out_shape=(jax.ShapeDtypeStruct(slab, F32), jax.Sh...]
where the time goes in v2:
time: 85.3 us; the launch traced here: 85.1 us
  Pallas kernels  76.5 us (90%)
  local copies, waits for them, and re-layouts  7.94 us (9%)
    pallas_call x1, Pallas kernels, step(): pl.pallas_call(kernel, out_shape=(jax.ShapeDtypeStruct(slab, F32), jax.Sh...  76.5 us
    unnamed x9, local copies, waits for them, and re-layouts  7.94 us

profile of v2, /device:TPU:1, one launch (start us, length us, event | category | flops | bytes accessed | tf_op | source)
XLA Modules:
  0.0 85.1 jit_solution(2585802005580620884)
XLA Ops:
  0.6 1.6 %copy.17 = f32[32,8,2,128]{3,1,2,0:T(8,128)} copy(bf16[32,8,2,128]{3,2,1,0:T(2,128)(2,1)} %bitcast.13) | data formatting | bytes 393216
  2.3 76.5 %step.1 = (f32[2,64,2048]{2,1,0:T(8,128)}, f32[2,64,2048]{2,1,0:T(8,128)}, bf16[256,16,128]{2,1,0:T(8,128)(2,1)}, bf16[256,256]{1,0:T(8,128)(2,1)}) custom-call(bf16[2,64,2048]{2,1,0:T(8,128)(2,1)} %refs_0_.1, f32[2,64,2048]{2,1,0:T(8,128)} %refs_1_.1, f32[2,64,2048]{2,1,0:T(8,128)} %refs_2_.1, f32[2,64,2048]{2,1,0:T(8,128)} %refs_3_.1, ...), custom_call_target="tpu_custom_call" | custom-call | tf_op jit(solution)/shard_map/step/pallas_call | solution.py:409
  78.7 0.0 copy-start
  78.8 0.0 copy-start.1
  78.8 2.4 %copy.22 = f32[2,64,2048]{2,1,0:T(8,128)} copy(f32[2,64,2048]{2,1,0:T(8,128)} %get-tuple-element.8) | data formatting | bytes 2097152
  81.2 2.3 %copy.23 = f32[2,64,2048]{2,1,0:T(8,128)} copy(f32[2,64,2048]{2,1,0:T(8,128)} %get-tuple-element.9) | data formatting | bytes 2097152
  83.4 0.0 copy-done
  83.5 1.0 %copy.24 = bf16[256,16,128]{2,1,0:T(8,128)(2,1)} copy(bf16[256,16,128]{2,1,0:T(8,128)(2,1)S(1)} %copy-done) | data formatting | bytes 2097152
  84.4 0.0 copy-done.1
  84.4 0.7 copy.25
Async XLA Ops:
  78.7 4.7 %copy-start = (bf16[256,16,128]{2,1,0:T(8,128)(2,1)S(1)}, bf16[256,16,128]{2,1,0:T(8,128)(2,1)}, u32[]{:S(2)}) copy-start(bf16[256,16,128]{2,1,0:T(8,128)(2,1)} %get-tuple-element.10) | copy-start | bytes 3145732
  78.8 5.7 %copy-start.1 = (bf16[256,256]{1,0:T(8,128)(2,1)S(1)}, bf16[256,256]{1,0:T(8,128)(2,1)}, u32[]{:S(2)}) copy-start(bf16[256,256]{1,0:T(8,128)(2,1)} %get-tuple-element.11) | copy-start | bytes 393220

commit v3 on v2

--- a/solution.py
+++ b/solution.py
@@ -54,7 +54,7 @@
     grad_h, master_h, first_h, second_h, resid_h, gain_h, query_h, cache_h, fresh_h, length_ref, table_ref,
     first_o, second_o, attended_o, act_ref,
     g_v, ma_v, m_v, v_v, gf, gain_v, a_v, b_v, b_swap, c_s, c_r, h_s, h_r,
-    p_s, p_r, t_s, t_r, s_g, q_v, kv_v, f_v, o_v, len_v, load_sem, sends, recvs, many,
+    p_s, p_r, t_s, t_r, s_g, q_v, kv_v, f_v, o_v, len_v, last, load_sem, sends, recvs, many,
 ):
     d = lax.axis_index("dp")
     t = lax.axis_index("tensor")
@@ -73,11 +73,15 @@
     to_xq, to_yq, to_zl = at(xq, zl, y), at(x, zl, yq), at(x, 1 - zl, y)
     to_core = at(x, zl, y, zh, oc)
 
-    barrier = pltpu.get_barrier_semaphore()
-    for k in range(1, 8):
-        pl.semaphore_signal(barrier, inc=1, device_id={"dp": d, "tensor": (t + k) % 8}, device_id_type=MESH)
-    for k in range(1, 32):
-        pl.semaphore_signal(barrier, inc=1, device_id={"dp": (d + k) % 32, "tensor": t}, device_id_type=MESH)
+    near = [
+        at(x_, z_, y_, zh, c_)
+        for x_ in (x, xp) for y_ in (y, yp) for z_ in (zl, 1 - zl) for c_ in (c, oc)
+    ][1:]
+    far = [
+        at(x_, 1 - zl if k == 2 else zl, y_, (zh + k) % 4, c)
+        for x_ in (x, xq) for y_ in (y, yq) for k in range(4)
+    ][1:]
+    team = [at(x, zl, y, (zh + k // 2) % 4, (c + k) % 2) for k in range(1, 8)]
 
     loads = [
         pltpu.make_async_copy(grad_h, g_v, load_sem.at[0]),
@@ -90,8 +94,11 @@
         pltpu.make_async_copy(fresh_h, f_v, load_sem.at[7]),
         pltpu.make_async_copy(cache_h, kv_v, load_sem.at[8]),
     ]
-    for load in loads:
-        load.start()
+    loads[0].start()
+    barrier = pltpu.get_barrier_semaphore()
+    greeted = near + far + [team[k] for k in (2, 3, 4, 6)]
+    for peer in greeted:
+        pl.semaphore_signal(barrier, inc=1, device_id=peer, device_id_type=MESH)
 
     used = []
 
@@ -101,6 +108,8 @@
         return r
 
     loads[0].wait()
+    for load in loads[1:]:
+        load.start()
 
     def square(i, acc):
         g = g_v[i // 4, pl.ds(pl.multiple_of((i % 4) * 16, 16), 16), :].astype(F32)
@@ -110,14 +119,24 @@
 
     acc = lax.fori_loop(0, 8, square, jnp.zeros((8, K_DEV), F32))
     local = jnp.sum(jnp.sum(acc, axis=0, keepdims=True), axis=1, keepdims=True)
-    p_s[...] = jnp.broadcast_to(local, (8, 128))
-
-    pl.semaphore_wait(barrier, 38)
-
-    for k in range(1, 32):
-        pltpu.make_async_remote_copy(
-            src_ref=p_s, dst_ref=p_r.at[k - 1], send_sem=many.at[0], recv_sem=many.at[1],
-            device_id={"dp": (d + k) % 32, "tensor": t}, device_id_type=MESH).start()
+    p_s[0] = jnp.broadcast_to(local, (8, 128))
+
+    pl.semaphore_wait(barrier, len(greeted))
+
+    def to_all(src, dst, peers, pair):
+        for k, peer in enumerate(peers):
+            pltpu.make_async_remote_copy(
+                src_ref=src, dst_ref=dst.at[k], send_sem=many.at[pair], recv_sem=many.at[pair + 1],
+                device_id=peer, device_id_type=MESH).start()
+
+    def from_all(dst, pair):
+        whole = pltpu.make_async_remote_copy(
+            src_ref=dst, dst_ref=dst, send_sem=many.at[pair], recv_sem=many.at[pair + 1],
+            device_id=to_core, device_id_type=MESH)
+        whole.wait_send()
+        whole.wait_recv()
+
+    to_all(p_s.at[0], p_r.at[0], near, 0)
 
     loads[1].wait()
     ones = jnp.ones((8, 512), BF16)
@@ -130,7 +149,7 @@
         for part in (high, low):
             row_squares += lax.dot_general(ones, part, (((1,), (1,)), ((), ())), preferred_element_type=F32)
 
-    t_s[:, 128:] = row_squares
+    t_s[...] = row_squares
 
     row8 = lax.broadcasted_iota(jnp.int32, (32, ROWS), 1)
     spread_len = jnp.where(
@@ -148,9 +167,8 @@
         q = q_v[rows].reshape(128, 128)
         keys = kv_v[rows, 0].reshape(256, 128)
         values = kv_v[rows, 1].reshape(256, 128)
-        own = f_v[rows, :]
-        own_key = jnp.broadcast_to(own[:, :128].reshape(8, 1, 128), (8, 16, 128)).reshape(128, 128)
-        own_value = jnp.broadcast_to(own[:, 128:].reshape(8, 1, 128), (8, 16, 128)).reshape(128, 128)
+        own_key = jnp.broadcast_to(f_v[rows, 0].astype(F32), (8, 16, 128)).reshape(128, 128)
+        own_value = jnp.broadcast_to(f_v[rows, 1].astype(F32), (8, 16, 128)).reshape(128, 128)
         head = lax.broadcasted_iota(jnp.int32, (128, 256), 0)
         pos = lax.broadcasted_iota(jnp.int32, (128, 256), 1)
         scores = lax.dot_general(q, keys, (((1,), (1,)), ((), ())), preferred_element_type=F32) * SCORE_SCALE
@@ -171,22 +189,13 @@
         def _(g):
             attend_block(g)
 
-    attend(0, 8)
-
-    everyone = pltpu.make_async_remote_copy(
-        src_ref=p_r, dst_ref=p_r, send_sem=many.at[0], recv_sem=many.at[1],
-        device_id=to_core, device_id_type=MESH)
-    everyone.wait_send()
-    everyone.wait_recv()
-    total = p_s[...]
-    for k in range(31):
-        total += p_r[k]
-    t_s[:, :128] = total
-
-    for k in range(1, 8):
-        pltpu.make_async_remote_copy(
-            src_ref=t_s, dst_ref=t_r.at[k - 1], send_sem=many.at[2], recv_sem=many.at[3],
-            device_id={"dp": d, "tensor": (t + k) % 8}, device_id_type=MESH).start()
+    from_all(p_r.at[0], 0)
+    total = p_s[0]
+    for k in range(15):
+        total += p_r[0, k]
+    p_s[1] = total
+    to_all(p_s.at[1], p_r.at[1], far, 2)
+    to_all(t_s, t_r, team, 4)
 
     def rows_of(slot, half, r):
         return a_v.at[slot, half, pl.ds(r * 128, 128)]
@@ -198,19 +207,13 @@
     rows_y = [remote(rows_of(0, c, r), rows_of(2, c, r), to_yp) for r in range(2)]
     core_rows = [to_other_core(0, 0), to_other_core(0, 1)]
 
-    attend(8, 18)
-
-    team = pltpu.make_async_remote_copy(
-        src_ref=t_r, dst_ref=t_r, send_sem=many.at[2], recv_sem=many.at[3],
-        device_id=to_core, device_id_type=MESH)
-    team.wait_send()
-    team.wait_recv()
-    both = t_s[...]
-    for k in range(7):
-        both += t_r[k]
-    clip = jnp.minimum(1.0, clip_limit / (jnp.sqrt(both[:, :128]) + CLIP_EPSILON))
-    s_g[0] = both[:, 128:]
-    square_copies = [remote(s_g.at[0], s_g.at[slot], device) for slot, device in ((1, to_xp), (2, to_yp), (3, to_diag))]
+    attend(0, 10)
+
+    from_all(p_r.at[1], 2)
+    total = p_s[1]
+    for k in range(15):
+        total += p_r[1, k]
+    clip = jnp.minimum(1.0, clip_limit / (jnp.sqrt(total) + CLIP_EPSILON))
 
     for load in loads[2:6]:
         load.wait()
@@ -262,7 +265,13 @@
     ]
     stores[0].start()
     stores[1].start()
-    attend(18, 32)
+    from_all(t_r, 4)
+    squares = t_s[...]
+    for k in range(7):
+        squares += t_r[k]
+    s_g[0] = squares
+    square_copies = [remote(s_g.at[0], s_g.at[slot], device) for slot, device in ((1, to_xp), (2, to_yp), (3, to_diag))]
+    attend(10, 32)
     stores[2].start()
 
     core_got = []
@@ -293,11 +302,12 @@
     for r in core_rows + core_got:
         r.came()
 
+    def half_product(slot, count, a, h):
+        lhs = b_v[slot:slot + count, h].reshape(count * UNITS, K_DEV)
+        return lax.dot_general(lhs, a_v[a, h], (((1,), (1,)), ((), ())), preferred_element_type=F32)
+
     def product(slot, count, a):
-        out = jnp.zeros((count * UNITS, ROWS), F32)
-        for h in range(2):
-            lhs = b_v[slot:slot + count, h].reshape(count * UNITS, K_DEV)
-            out += lax.dot_general(lhs, a_v[a, h], (((1,), (1,)), ((), ())), preferred_element_type=F32)
+        out = half_product(slot, count, a, 0) + half_product(slot, count, a, 1)
         return out.reshape(count, 4, 16, ROWS).astype(BF16)
 
     def pair_tile(p, a):
@@ -338,38 +348,16 @@
         pair_tile(p, 3)
     send_sums(lambda z: c_s.at[pl.ds(0, 3), z, 3], lambda k: c_r.at[k, pl.ds(0, 3), 3])
 
-    for q in range(2):
-        for k in range(2):
-            unit[6 + q, k].came()
-
-        @pl.loop(0, 4)
-        def _(a):
-            out = product(6 + q, 1, a)
-            for z in range(4):
-                c_s[3, z, a, q] = out[0, z]
-
-        send_sums(lambda z: c_s.at[3, z, :, q], lambda k: c_r.at[k, 3, :, q])
-
-    for r in square_copies:
-        r.came()
-    for r in sums:
-        r.came()
-    outs = []
-    for a, device in ((1, to_xp), (2, to_yp), (3, to_diag), (0, None)):
-        scale = lax.rsqrt(s_g[a][0:1, :] * (1.0 / WIDTH) + NORM_EPSILON)
-        for p in range(4):
-            v = c_s[p, zh, a].astype(F32)
-            for k in range(3):
-                v += c_r[k, p, a].astype(F32)
-            gate = v[:, :8] * scale
-            up = v[:, 8:] * scale
-            hidden = (gate / (1.0 + jnp.exp(-gate)) * up).reshape(16, ROWS).astype(BF16)
-            if device is None:
-                h_r[0, p * 16:(p + 1) * 16, :] = hidden
-            else:
-                h_s[a - 1, p * 16:(p + 1) * 16, :] = hidden
-        if device is not None:
-            outs.append(remote(h_s.at[a - 1], h_r.at[a], device))
+    for k in range(2):
+        unit[6, k].came()
+
+    @pl.loop(0, 4)
+    def _(a):
+        out = product(6, 1, a)
+        for z in range(4):
+            c_s[3, z, a, 0] = out[0, z]
+
+    send_sums(lambda z: c_s.at[3, z, :, 0], lambda k: c_r.at[k, 3, :, 0])
 
     u = lax.broadcasted_iota(jnp.int32, (256, 256), 0)
     col = lax.broadcasted_iota(jnp.int32, (256, 256), 1)
@@ -385,6 +373,48 @@
     table = jnp.broadcast_to(table_ref[...].astype(F32), (8, 32)).astype(BF16)
     wanted = jnp.dot(table, spread, preferred_element_type=F32)[0:1, :].astype(jnp.int32)
     pick = jnp.where((shard == wanted) & (u % 8 == col % 8), 1.0, 0.0).astype(BF16)
+    unit[7, 0].came()
+
+    @pl.loop(0, 4)
+    def _(a):
+        last[a] = half_product(7, 1, a, c)
+
+    unit[7, 1].came()
+
+    @pl.loop(0, 4)
+    def _(a):
+        out = (last[a] + half_product(7, 1, a, oc)).reshape(4, 16, ROWS).astype(BF16)
+        for z in range(4):
+            c_s[3, z, a, 1] = out[z]
+
+    send_sums(lambda z: c_s.at[3, z, :, 1], lambda k: c_r.at[k, 3, :, 1])
+
+    for r in square_copies:
+        r.came()
+
+    def activations(a, p):
+        scale = lax.rsqrt(s_g[a][0:1, :] * (1.0 / WIDTH) + NORM_EPSILON)
+        v = c_s[p, zh, a].astype(F32)
+        for k in range(3):
+            v += c_r[k, p, a].astype(F32)
+        gate = v[:, :8] * scale
+        up = v[:, 8:] * scale
+        hidden = (gate / (1.0 + jnp.exp(-gate)) * up).reshape(16, ROWS).astype(BF16)
+        h_s[a, p * 16:(p + 1) * 16, :] = hidden
+
+    for r in sums[:12]:
+        r.came()
+    for a in range(4):
+        for p in range(3):
+            activations(a, p)
+    for r in sums[12:]:
+        r.came()
+    outs = []
+    for a, device in ((3, to_diag), (1, to_xp), (2, to_yp)):
+        activations(a, 3)
+        outs.append(remote(h_s.at[a], h_r.at[a], device))
+    activations(0, 3)
+    h_r[0] = h_s[0]
     for r in outs:
         r.came()
     act_ref[...] = lax.dot_general(
@@ -406,7 +436,7 @@
     def kernel(*refs):
         step_kernel(clip_limit, *refs)
 
-    return pl.pallas_call(
+    results = pl.pallas_call(
         kernel,
         out_shape=(
             jax.ShapeDtypeStruct(slab, F32),
@@ -428,29 +458,46 @@
             pltpu.VMEM((UNITS, K_DEV), BF16),
             pltpu.VMEM((4, 4, 4, 2, 16, ROWS), BF16),
             pltpu.VMEM((3, 4, 4, 2, 16, ROWS), BF16),
-            pltpu.VMEM((3, UNITS, ROWS), BF16),
             pltpu.VMEM((4, UNITS, ROWS), BF16),
-            pltpu.VMEM((8, 128), F32),
-            pltpu.VMEM((31, 8, 128), F32),
-            pltpu.VMEM((8, 384), F32),
-            pltpu.VMEM((7, 8, 384), F32),
+            pltpu.VMEM((4, UNITS, ROWS), BF16),
+            pltpu.VMEM((2, 8, 128), F32),
+            pltpu.VMEM((2, 15, 8, 128), F32),
+            pltpu.VMEM((8, ROWS), F32),
+            pltpu.VMEM((7, 8, ROWS), F32),
             pltpu.VMEM((4, 8, ROWS), F32),
             pltpu.VMEM(queries.shape, BF16),
             pltpu.VMEM((ROWS, 2, 32, 128), BF16),
-            pltpu.VMEM((ROWS, 256), F32),
+            pltpu.VMEM(fresh_entries.shape, BF16),
             pltpu.VMEM(queries.shape, BF16),
             pltpu.VMEM((32, 256), F32),
+            pltpu.VMEM((4, UNITS, ROWS), F32),
             pltpu.SemaphoreType.DMA((12,)),
             pltpu.SemaphoreType.DMA((N_COPIES,)),
             pltpu.SemaphoreType.DMA((N_COPIES,)),
-            pltpu.SemaphoreType.DMA((4,)),
+            pltpu.SemaphoreType.DMA((6,)),
         ],
         compiler_params=pltpu.CompilerParams(
             collective_id=0, has_side_effects=True, vmem_limit_bytes=56 << 20),
         name="step",
     )(gradient, master, first_moment, second_moment, residual,
       norm_gain.reshape(128, 128), queries, layer_cache.reshape(ROWS, 2, 32, 128),
-      fresh_entries.astype(F32).reshape(ROWS, 256), lengths.reshape(1, ROWS), shard_table.reshape(1, 32))
+      fresh_entries, lengths.reshape(1, ROWS), shard_table.reshape(1, 32))
+
+    def write(*refs):
+        copies = [pltpu.make_async_copy(refs[i], refs[4 + i], refs[8].at[i]) for i in range(4)]
+        for copy in copies:
+            copy.start()
+        for copy in copies:
+            copy.wait()
+
+    return pl.pallas_call(
+        write,
+        out_shape=[jax.ShapeDtypeStruct(r.shape, r.dtype) for r in results],
+        in_specs=[hbm] * 4,
+        out_specs=[hbm] * 4,
+        scratch_shapes=[pltpu.SemaphoreType.DMA((4,))],
+        name="write",
+    )(*results)
 
 
 def per_device(gradient, master, first_moment, second_moment, residual, norm_gain,

time: 85.3 us -> 180 us (2.11)
  Pallas kernels: 76.5 us -> 178 us
  local copies, waits for them, and re-layouts: 7.94 us -> 1.79 us
    pallas_call x0 -> x1, Pallas kernels: none -> 100 us  [step(): pl.pallas_call(write, out_shape=[jax.ShapeDtypeStruct(r.shape, r.dtype) f...]
    unnamed x9 -> x1, local copies, waits for them, and re-layouts: 7.94 us -> 1.79 us
where the time goes in v3:
time: 180 us
  Pallas kernels  178 us (99%)
    pallas_call x1, Pallas kernels, step(): pl.pallas_call(write, out_shape=[jax.ShapeDtypeStruct(r.shape, r.dtype) f...  100 us
    pallas_call x1, Pallas kernels, step(): pl.pallas_call(kernel, out_shape=(jax.ShapeDtypeStruct(slab, F32), jax.Sh...  77.1 us

profile of v3, /device:TPU:1, one launch (start us, length us, event | category | flops | bytes accessed | tf_op | source)
XLA Modules:
  0.0 179.9 jit_solution(10824253759978379479)
XLA Ops:
  0.6 1.8 copy.15.refs_8_
  2.4 77.1 %step.1 = (f32[2,64,2048]{2,1,0:T(8,128)}, f32[2,64,2048]{2,1,0:T(8,128)}, bf16[256,16,128]{2,1,0:T(8,128)(2,1)}, bf16[256,256]{1,0:T(8,128)(2,1)}) custom-call(bf16[2,64,2048]{2,1,0:T(8,128)(2,1)} %refs_0_.1, f32[2,64,2048]{2,1,0:T(8,128)} %refs_1_.1, f32[2,64,2048]{2,1,0:T(8,128)} %refs_2_.1, f32[2,64,2048]{2,1,0:T(8,128)} %refs_3_.1, ...), custom_call_target="tpu_custom_call" | custom-call | tf_op jit(solution)/shard_map/step/pallas_call | solution.py:439
  79.5 100.4 %write.1 = (f32[2,64,2048]{2,1,0:T(8,128)}, f32[2,64,2048]{2,1,0:T(8,128)}, bf16[256,16,128]{2,1,0:T(8,128)(2,1)}, bf16[256,256]{1,0:T(8,128)(2,1)}) custom-call(f32[2,64,2048]{2,1,0:T(8,128)} %get-tuple-element.8.refs_0_, f32[2,64,2048]{2,1,0:T(8,128)} %get-tuple-element.9.refs_1_, bf16[256,16,128]{2,1,0:T(8,128)(2,1)} %get-tuple-element.10.refs_2_, ...), custom_call_target="tpu_custom_call" | custom-call | tf_op jit(solution)/shard_map/write/pallas_call | solution.py:493

commit v4 on v3

--- a/solution.py
+++ b/solution.py
@@ -54,7 +54,7 @@
     grad_h, master_h, first_h, second_h, resid_h, gain_h, query_h, cache_h, fresh_h, length_ref, table_ref,
     first_o, second_o, attended_o, act_ref,
     g_v, ma_v, m_v, v_v, gf, gain_v, a_v, b_v, b_swap, c_s, c_r, h_s, h_r,
-    p_s, p_r, t_s, t_r, s_g, q_v, kv_v, f_v, o_v, len_v, last, load_sem, sends, recvs, many,
+    p_s, p_r, t_s, t_r, s_g, q_v, kv_v, f_v, len_v, last, pick, load_sem, sends, recvs, many,
 ):
     d = lax.axis_index("dp")
     t = lax.axis_index("tensor")
@@ -95,6 +95,7 @@
         pltpu.make_async_copy(cache_h, kv_v, load_sem.at[8]),
     ]
     loads[0].start()
+    loads[1].start()
     barrier = pltpu.get_barrier_semaphore()
     greeted = near + far + [team[k] for k in (2, 3, 4, 6)]
     for peer in greeted:
@@ -108,7 +109,7 @@
         return r
 
     loads[0].wait()
-    for load in loads[1:]:
+    for load in loads[2:]:
         load.start()
 
     def square(i, acc):
@@ -139,6 +140,69 @@
     to_all(p_s.at[0], p_r.at[0], near, 0)
 
     loads[1].wait()
+    def rows_of(slot, half, r):
+        return a_v.at[slot, half, pl.ds(r * 128, 128)]
+
+    def to_other_core(slot, r):
+        return remote(rows_of(slot, c, r), rows_of(slot, c, r), to_core, rows_of(slot, oc, r))
+
+    rows_x = [remote(rows_of(0, c, r), rows_of(1, c, r), to_xp) for r in range(2)]
+    rows_y = [remote(rows_of(0, c, r), rows_of(2, c, r), to_yp) for r in range(2)]
+    core_rows = [to_other_core(0, 0), to_other_core(0, 1)]
+
+    own_len = jnp.where(
+        lax.broadcasted_iota(jnp.int32, (32, ROWS), 1) // 8
+        == lax.broadcasted_iota(jnp.int32, (32, ROWS), 0),
+        jnp.broadcast_to(length_ref[...].astype(F32), (32, ROWS)), 0.0).astype(BF16)
+    spread_len = jnp.where(
+        lax.broadcasted_iota(jnp.int32, (ROWS, 128), 0) % 8
+        == lax.broadcasted_iota(jnp.int32, (ROWS, 128), 1) // 16, 1.0, 0.0).astype(BF16)
+    len_v[...] = jnp.dot(own_len, spread_len, preferred_element_type=F32)
+
+    def attend_block(g):
+        rows = pl.ds(pl.multiple_of(g * 8, 8), 8)
+        lane_row = lax.broadcasted_iota(jnp.int32, (32, 128), 1) // 16
+        position = lax.broadcasted_iota(jnp.int32, (32, 128), 0).astype(F32)
+        own_mine = (lax.broadcasted_iota(jnp.int32, (16, 128), 0)
+                    == lax.broadcasted_iota(jnp.int32, (16, 128), 1) // 16)
+        q = q_v[rows].reshape(128, 128)
+        keys = kv_v[rows, 0].reshape(256, 128)
+        values = kv_v[rows, 1].reshape(256, 128)
+        own_key = f_v[rows, 0, 0:1].astype(F32).reshape(8, 128)
+        own_value = f_v[rows, 0, 1:2].astype(F32).reshape(8, 128)
+        own_key = jnp.concatenate([own_key, own_key], axis=0).astype(BF16)
+        own_value = jnp.concatenate([own_value, own_value], axis=0).astype(BF16)
+        every = lax.dot_general(keys, q, (((1,), (1,)), ((), ())), preferred_element_type=F32)
+        own = lax.dot_general(own_key, q, (((1,), (1,)), ((), ())), preferred_element_type=F32)
+        scores = every[:32]
+        for r in range(1, 8):
+            scores = jnp.where(lane_row == r, every[32 * r:32 * r + 32], scores)
+        scores = jnp.where(position < len_v[pl.ds(g, 1), :], scores * SCORE_SCALE, -jnp.inf)
+        own = jnp.sum(jnp.where(own_mine, own, 0.0), axis=0, keepdims=True) * SCORE_SCALE
+        peak = jnp.maximum(jnp.max(scores, axis=0, keepdims=True), own)
+        cached = jnp.exp(scores - peak)
+        fresh_exp = jnp.exp(own - peak)
+        inverse = 1.0 / (jnp.sum(cached, axis=0, keepdims=True) + fresh_exp)
+        prob = cached * inverse
+        own_prob = jnp.where(own_mine, fresh_exp * inverse, 0.0).astype(BF16)
+        wide = jnp.concatenate([jnp.where(lane_row == r, prob, 0.0) for r in range(8)], axis=0).astype(BF16)
+        out = lax.dot_general(wide, values, (((0,), (0,)), ((), ())), preferred_element_type=F32)
+        out += lax.dot_general(own_prob, own_value, (((0,), (0,)), ((), ())), preferred_element_type=F32)
+        attended_o[rows] = out.astype(BF16).reshape(8, 16, 128)
+
+    def attend(first, last):
+        @pl.loop(first // 4, last // 4)
+        def _(g):
+            for i in range(4):
+                attend_block(4 * g + i)
+
+    from_all(p_r.at[0], 0)
+    total = p_s[0]
+    for k in range(15):
+        total += p_r[0, k]
+    p_s[1] = total
+    to_all(p_s.at[1], p_r.at[1], far, 2)
+
     ones = jnp.ones((8, 512), BF16)
     row_squares = jnp.zeros((8, ROWS), F32)
     for k in range(4):
@@ -150,64 +214,11 @@
             row_squares += lax.dot_general(ones, part, (((1,), (1,)), ((), ())), preferred_element_type=F32)
 
     t_s[...] = row_squares
-
-    row8 = lax.broadcasted_iota(jnp.int32, (32, ROWS), 1)
-    spread_len = jnp.where(
-        lax.broadcasted_iota(jnp.int32, (ROWS, 256), 0) % 8
-        == lax.broadcasted_iota(jnp.int32, (ROWS, 256), 1) // 32, 1.0, 0.0).astype(BF16)
-    own_len = jnp.where(
-        row8 // 8 == lax.broadcasted_iota(jnp.int32, (32, ROWS), 0),
-        jnp.broadcast_to(length_ref[...].astype(F32), (32, ROWS)), 0.0).astype(BF16)
-    len_v[...] = jnp.dot(own_len, spread_len, preferred_element_type=F32)
+    to_all(t_s, t_r, team, 4)
+
     for load in loads[6:]:
         load.wait()
-
-    def attend_block(g):
-        rows = pl.ds(pl.multiple_of(g * 8, 8), 8)
-        q = q_v[rows].reshape(128, 128)
-        keys = kv_v[rows, 0].reshape(256, 128)
-        values = kv_v[rows, 1].reshape(256, 128)
-        own_key = jnp.broadcast_to(f_v[rows, 0].astype(F32), (8, 16, 128)).reshape(128, 128)
-        own_value = jnp.broadcast_to(f_v[rows, 1].astype(F32), (8, 16, 128)).reshape(128, 128)
-        head = lax.broadcasted_iota(jnp.int32, (128, 256), 0)
-        pos = lax.broadcasted_iota(jnp.int32, (128, 256), 1)
-        scores = lax.dot_general(q, keys, (((1,), (1,)), ((), ())), preferred_element_type=F32) * SCORE_SCALE
-        own_score = jnp.sum(q.astype(F32) * own_key, axis=1, keepdims=True) * SCORE_SCALE
-        valid = (head // 16 == pos // 32) & ((pos % 32).astype(F32) < len_v[pl.ds(g, 1), :])
-        scores = jnp.where(valid, scores, -jnp.inf)
-        peak = jnp.maximum(jnp.max(scores, axis=1, keepdims=True), own_score)
-        cached = jnp.exp(scores - peak)
-        fresh_exp = jnp.exp(own_score - peak)
-        inverse = 1.0 / (jnp.sum(cached, axis=1, keepdims=True) + fresh_exp)
-        prob = (cached * inverse).astype(BF16)
-        own_prob = (fresh_exp * inverse).astype(BF16).astype(F32)
-        out = jnp.dot(prob, values, preferred_element_type=F32) + own_prob * own_value
-        o_v[rows] = out.astype(BF16).reshape(8, 16, 128)
-
-    def attend(first, last):
-        @pl.loop(first, last)
-        def _(g):
-            attend_block(g)
-
-    from_all(p_r.at[0], 0)
-    total = p_s[0]
-    for k in range(15):
-        total += p_r[0, k]
-    p_s[1] = total
-    to_all(p_s.at[1], p_r.at[1], far, 2)
-    to_all(t_s, t_r, team, 4)
-
-    def rows_of(slot, half, r):
-        return a_v.at[slot, half, pl.ds(r * 128, 128)]
-
-    def to_other_core(slot, r):
-        return remote(rows_of(slot, c, r), rows_of(slot, c, r), to_core, rows_of(slot, oc, r))
-
-    rows_x = [remote(rows_of(0, c, r), rows_of(1, c, r), to_xp) for r in range(2)]
-    rows_y = [remote(rows_of(0, c, r), rows_of(2, c, r), to_yp) for r in range(2)]
-    core_rows = [to_other_core(0, 0), to_other_core(0, 1)]
-
-    attend(0, 10)
+    attend(0, 8)
 
     from_all(p_r.at[1], 2)
     total = p_s[1]
@@ -229,8 +240,8 @@
             new_second = SECOND_DECAY * v_v[i, pl.ds(row, 8), :] + (1.0 - SECOND_DECAY) * clipped * clipped
             step = (new_first * (LEARN_RATE / FIRST_CORRECTION)) / (
                 jnp.sqrt(new_second * (1.0 / SECOND_CORRECTION)) + ADAM_EPSILON)
-            m_v[i, pl.ds(row, 8), :] = new_first
-            v_v[i, pl.ds(row, 8), :] = new_second
+            first_o[i, pl.ds(row, 8), :] = new_first
+            second_o[i, pl.ds(row, 8), :] = new_second
             parts.append((ma_v[i, pl.ds(row, 8), :] - step) * gain)
         return jnp.concatenate(parts, axis=0).astype(BF16)
 
@@ -244,11 +255,9 @@
     def _(zone):
         b_v[0, c, pl.ds(pl.multiple_of(zone * 16, 16), 16), :] = fresh(c, zone)
 
-    def piece(slot, k):
-        return b_v.at[slot, c if k == 0 else oc]
-
     def units(src, dst, k, device):
-        return remote(piece(src, k), piece(dst, k), device)
+        half = c if k == 0 else oc
+        return remote(b_v.at[src, half], b_v.at[dst, half], device)
 
     unit = {}
     for k in range(2):
@@ -256,23 +265,34 @@
             swap.came()
         unit[1, k] = units(0, 1, k, to_zl)
         unit[2, k] = units(0, 2, k, to_xq)
-        unit[4, k] = units(0, 4, k, to_yq)
-
-    stores = [
-        pltpu.make_async_copy(m_v, first_o, load_sem.at[9]),
-        pltpu.make_async_copy(v_v, second_o, load_sem.at[10]),
-        pltpu.make_async_copy(o_v, attended_o, load_sem.at[11]),
-    ]
-    stores[0].start()
-    stores[1].start()
+        unit[3, k] = units(0, 3, k, to_yq)
+
+    spread = (lax.broadcasted_iota(jnp.int32, (32, 256), 0)
+              == lax.broadcasted_iota(jnp.int32, (32, 256), 1) // 8).astype(F32).astype(BF16)
+    table = jnp.broadcast_to(table_ref[...].astype(F32), (8, 32)).astype(BF16)
+    wanted = jnp.dot(table, spread, preferred_element_type=F32)
+    same_unit = (lax.broadcasted_iota(jnp.int32, (8, 256), 0)
+                 == lax.broadcasted_iota(jnp.int32, (8, 256), 1) % 8)
+    for group in range(4):
+        gx, gy = (xp if group % 2 else x), (yp if group // 2 else y)
+        for pair in range(4):
+            halves = []
+            for block in (2 * pair, 2 * pair + 1):
+                bx = (gx + 3 + 2 * (gx % 2)) % 4 if block in (2, 4, 6, 7) else gx
+                by = (gy + 3 + 2 * (gy % 2)) % 4 if block in (3, 5, 6, 7) else gy
+                bz = 1 - zl if block in (1, 4, 5, 7) else zl
+                shard = (bx * 8 + bz * 4 + by).astype(F32)
+                halves.append(jnp.where(same_unit & (wanted == shard), 1.0, 0.0))
+            row = group * 64 + pair * 16
+            pick[row:row + 16, :] = jnp.concatenate(halves, axis=0).astype(BF16)
+
     from_all(t_r, 4)
     squares = t_s[...]
     for k in range(7):
         squares += t_r[k]
     s_g[0] = squares
     square_copies = [remote(s_g.at[0], s_g.at[slot], device) for slot, device in ((1, to_xp), (2, to_yp), (3, to_diag))]
-    attend(10, 32)
-    stores[2].start()
+    attend(8, 32)
 
     core_got = []
     diag = []
@@ -290,13 +310,13 @@
     pass_rows(0)
     for k in range(2):
         unit[1, k].came()
-        unit[3, k] = units(1, 3, k, to_xq)
+        unit[4, k] = units(1, 4, k, to_xq)
         unit[5, k] = units(1, 5, k, to_yq)
     unit[2, 0].came()
     unit[6, 0] = units(2, 6, 0, to_yq)
-    unit[4, 0].came()
-    unit[4, 1].came()
-    unit[6, 1] = units(4, 6, 1, to_xq)
+    unit[3, 0].came()
+    unit[3, 1].came()
+    unit[6, 1] = units(3, 6, 1, to_xq)
     unit[2, 1].came()
     pass_rows(1)
     for r in core_rows + core_got:
@@ -310,10 +330,11 @@
         out = half_product(slot, count, a, 0) + half_product(slot, count, a, 1)
         return out.reshape(count, 4, 16, ROWS).astype(BF16)
 
-    def pair_tile(p, a):
-        out = product(2 * p, 2, a)
-        for z in range(4):
-            c_s[p, z, a] = out[:, z]
+    def tile(p, pairs, a):
+        out = product(2 * p, 2 * pairs, a)
+        for i in range(pairs):
+            for z in range(4):
+                c_s[p + i, z, a] = out[2 * i:2 * i + 2, z]
 
     sums = []
 
@@ -322,30 +343,31 @@
             z = (zh + k) % 4
             sums.append(remote(view_s(z), view_r(k - 1), at(x, zl, y, z, c)))
 
-    def pair_three(p):
-        @pl.loop(0, 3)
-        def _(a):
-            pair_tile(p, a)
-
-        send_sums(lambda z: c_s.at[p, z, pl.ds(0, 3)], lambda k: c_r.at[k, p, pl.ds(0, 3)])
-
-    pair_three(0)
-    unit[3, 0].came()
-    unit[7, 0] = units(3, 7, 0, to_yq)
+    @pl.loop(0, 3)
+    def _(a):
+        tile(0, 2, a)
+
+    send_sums(lambda z: c_s.at[pl.ds(0, 2), z, pl.ds(0, 3)], lambda k: c_r.at[k, pl.ds(0, 2), pl.ds(0, 3)])
+    unit[4, 0].came()
+    unit[7, 0] = units(4, 7, 0, to_yq)
     unit[5, 0].came()
     unit[5, 1].came()
     unit[7, 1] = units(5, 7, 1, to_xq)
-    unit[3, 1].came()
-    pair_three(1)
-    pair_three(2)
+    unit[4, 1].came()
+
+    @pl.loop(0, 3)
+    def _(a):
+        tile(2, 1, a)
+
+    send_sums(lambda z: c_s.at[2, z, pl.ds(0, 3)], lambda k: c_r.at[k, 2, pl.ds(0, 3)])
     last_rows = []
     for r in range(2):
         diag[r].came()
         last_rows.append(to_other_core(3, r))
     for r in last_rows:
         r.came()
-    for p in range(3):
-        pair_tile(p, 3)
+    tile(0, 2, 3)
+    tile(2, 1, 3)
     send_sums(lambda z: c_s.at[pl.ds(0, 3), z, 3], lambda k: c_r.at[k, pl.ds(0, 3), 3])
 
     for k in range(2):
@@ -359,20 +381,6 @@
 
     send_sums(lambda z: c_s.at[3, z, :, 0], lambda k: c_r.at[k, 3, :, 0])
 
-    u = lax.broadcasted_iota(jnp.int32, (256, 256), 0)
-    col = lax.broadcasted_iota(jnp.int32, (256, 256), 1)
-    slot, pair, zbit = u // 64, (u // 16) % 4, (u // 8) % 2
-    xs = jnp.where(slot % 2 == 1, xp, x)
-    ys = jnp.where(slot // 2 == 1, yp, y)
-    xs = jnp.where(pair % 2 == 1, (xs + 3 + 2 * (xs % 2)) % 4, xs)
-    ys = jnp.where(pair // 2 == 1, (ys + 3 + 2 * (ys % 2)) % 4, ys)
-    zs = jnp.where(zbit == 1, 1 - zl, zl)
-    shard = xs * 8 + zs * 4 + ys
-    spread = (lax.broadcasted_iota(jnp.int32, (32, 256), 0)
-              == lax.broadcasted_iota(jnp.int32, (32, 256), 1) // 8).astype(F32).astype(BF16)
-    table = jnp.broadcast_to(table_ref[...].astype(F32), (8, 32)).astype(BF16)
-    wanted = jnp.dot(table, spread, preferred_element_type=F32)[0:1, :].astype(jnp.int32)
-    pick = jnp.where((shard == wanted) & (u % 8 == col % 8), 1.0, 0.0).astype(BF16)
     unit[7, 0].came()
 
     @pl.loop(0, 4)
@@ -402,12 +410,12 @@
         hidden = (gate / (1.0 + jnp.exp(-gate)) * up).reshape(16, ROWS).astype(BF16)
         h_s[a, p * 16:(p + 1) * 16, :] = hidden
 
-    for r in sums[:12]:
+    for r in sums[:9]:
         r.came()
     for a in range(4):
         for p in range(3):
             activations(a, p)
-    for r in sums[12:]:
+    for r in sums[9:]:
         r.came()
     outs = []
     for a, device in ((3, to_diag), (1, to_xp), (2, to_yp)):
@@ -418,10 +426,8 @@
     for r in outs:
         r.came()
     act_ref[...] = lax.dot_general(
-        h_r[...].reshape(256, ROWS), pick, (((0,), (0,)), ((), ())), preferred_element_type=F32).astype(BF16)
-
-    for store in stores:
-        store.wait()
+        h_r[...].reshape(256, ROWS), pick[...], (((0,), (0,)), ((), ())), preferred_element_type=F32).astype(BF16)
+
     for r in used:
         r.sent()
     assert len(used) <= N_COPIES, len(used)
@@ -439,13 +445,13 @@
     results = pl.pallas_call(
         kernel,
         out_shape=(
-            jax.ShapeDtypeStruct(slab, F32),
-            jax.ShapeDtypeStruct(slab, F32),
-            jax.ShapeDtypeStruct(queries.shape, BF16),
-            jax.ShapeDtypeStruct((ROWS, 256), BF16),
+            pltpu.VMEM(slab, F32),
+            pltpu.VMEM(slab, F32),
+            pltpu.VMEM(queries.shape, BF16),
+            pltpu.VMEM((ROWS, 256), BF16),
         ),
         in_specs=[hbm] * 9 + [vmem] * 2,
-        out_specs=(hbm, hbm, hbm, vmem),
+        out_specs=(vmem,) * 4,
         scratch_shapes=[
             pltpu.VMEM(slab, BF16),
             pltpu.VMEM(slab, F32),
@@ -467,11 +473,11 @@
             pltpu.VMEM((4, 8, ROWS), F32),
             pltpu.VMEM(queries.shape, BF16),
             pltpu.VMEM((ROWS, 2, 32, 128), BF16),
-            pltpu.VMEM(fresh_entries.shape, BF16),
-            pltpu.VMEM(queries.shape, BF16),
-            pltpu.VMEM((32, 256), F32),
+            pltpu.VMEM((ROWS, 1, 2, 128), BF16),
+            pltpu.VMEM((32, 128), F32),
             pltpu.VMEM((4, UNITS, ROWS), F32),
-            pltpu.SemaphoreType.DMA((12,)),
+            pltpu.VMEM((256, 256), BF16),
+            pltpu.SemaphoreType.DMA((9,)),
             pltpu.SemaphoreType.DMA((N_COPIES,)),
             pltpu.SemaphoreType.DMA((N_COPIES,)),
             pltpu.SemaphoreType.DMA((6,)),
@@ -481,7 +487,7 @@
         name="step",
     )(gradient, master, first_moment, second_moment, residual,
       norm_gain.reshape(128, 128), queries, layer_cache.reshape(ROWS, 2, 32, 128),
-      fresh_entries, lengths.reshape(1, ROWS), shard_table.reshape(1, 32))
+      fresh_entries.transpose(0, 2, 1, 3), lengths.reshape(1, ROWS), shard_table.reshape(1, 32))
 
     def write(*refs):
         copies = [pltpu.make_async_copy(refs[i], refs[4 + i], refs[8].at[i]) for i in range(4)]
@@ -493,11 +499,11 @@
     return pl.pallas_call(
         write,
         out_shape=[jax.ShapeDtypeStruct(r.shape, r.dtype) for r in results],
-        in_specs=[hbm] * 4,
+        in_specs=[vmem] * 4,
         out_specs=[hbm] * 4,
         scratch_shapes=[pltpu.SemaphoreType.DMA((4,))],
         name="write",
-    )(*results)
+    )(*[pltpu.with_memory_space_constraint(r, pltpu.VMEM) for r in results])
 
 
 def per_device(gradient, master, first_moment, second_moment, residual, norm_gain,

time: 180 us -> 74.5 us (0.41)
  Pallas kernels: 178 us -> 73.4 us
    pallas_call x1, Pallas kernels: 100 us -> 1.73 us  [step(): pl.pallas_call(write, out_shape=[jax.ShapeDtypeStruct(r.shape, r.dtype) f...]
    pallas_call x1, Pallas kernels: 77.1 us -> 71.7 us  [step(): pl.pallas_call(kernel, out_shape=(pltpu.VMEM(slab, F32), pltpu.VMEM(slab,...]
where the time goes in v4:
time: 74.5 us; the launch traced here: 74.1 us
  Pallas kernels  73.4 us (99%)
    pallas_call x1, Pallas kernels, step(): pl.pallas_call(kernel, out_shape=(pltpu.VMEM(slab, F32), pltpu.VMEM(slab,...  71.7 us
    pallas_call x1, Pallas kernels, step(): pl.pallas_call(write, out_shape=[jax.ShapeDtypeStruct(r.shape, r.dtype) f...  1.73 us

profile of v4, /device:TPU:1, one launch (start us, length us, event | category | flops | bytes accessed | tf_op | source)
XLA Modules:
  0.0 74.1 jit_solution(10542305041361678329)
XLA Ops:
  0.6 71.7 %step.1 = (f32[2,64,2048]{2,1,0:T(8,128)S(1)}, f32[2,64,2048]{2,1,0:T(8,128)S(1)}, bf16[256,16,128]{2,1,0:T(8,128)(2,1)S(1)}, bf16[256,256]{1,0:T(8,128)(2,1)S(1)}) custom-call(bf16[2,64,2048]{2,1,0:T(8,128)(2,1)} %refs_0_.1, f32[2,64,2048]{2,1,0:T(8,128)} %refs_1_.1, f32[2,64,2048]{2,1,0:T(8,128)} %refs_2_.1, f32[2,64,2048]{2,1,0:T(8,128)} %refs_3_.1, ...), custom_call_target="tpu_custom_call" | custom-call | tf_op jit(solution)/shard_map/step/pallas_call | solution.py:445
  72.3 1.7 %write.1 = (f32[2,64,2048]{2,1,0:T(8,128)}, f32[2,64,2048]{2,1,0:T(8,128)}, bf16[256,16,128]{2,1,0:T(8,128)(2,1)}, bf16[256,256]{1,0:T(8,128)(2,1)}) custom-call(f32[2,64,2048]{2,1,0:T(8,128)S(1)} %get-tuple-element.8.refs_0_, f32[2,64,2048]{2,1,0:T(8,128)S(1)} %get-tuple-element.9.refs_1_, bf16[256,16,128]{2,1,0:T(8,128)(2,1)S(1)} %get-tuple-element.10.refs_2_, ...), custom_call_target="tpu_custom_call" | custom-call | tf_op jit(solution)/shard_map/write/pallas_call | solution.py:499

commit v5 on v4

--- a/solution.py
+++ b/solution.py
@@ -51,10 +51,10 @@
 
 def step_kernel(
     clip_limit,
-    grad_h, master_h, first_h, second_h, resid_h, gain_h, query_h, cache_h, fresh_h, length_ref, table_ref,
+    grad_h, master_h, first_h, second_h, resid_h, gain_h, query_h, cache_h, fresh_h, length_h, table_h,
     first_o, second_o, attended_o, act_ref,
     g_v, ma_v, m_v, v_v, gf, gain_v, a_v, b_v, b_swap, c_s, c_r, h_s, h_r,
-    p_s, p_r, t_s, t_r, s_g, q_v, kv_v, f_v, len_v, last, pick, load_sem, sends, recvs, many,
+    p_s, p_r, t_s, t_r, s_g, q_v, kv_v, f_v, len_v, last, pick, length_ref, table_ref, load_sem, quarter_sem, sends, recvs, many,
 ):
     d = lax.axis_index("dp")
     t = lax.axis_index("tensor")
@@ -84,7 +84,7 @@
     team = [at(x, zl, y, (zh + k // 2) % 4, (c + k) % 2) for k in range(1, 8)]
 
     loads = [
-        pltpu.make_async_copy(grad_h, g_v, load_sem.at[0]),
+        None,
         pltpu.make_async_copy(resid_h, a_v.at[0, c], load_sem.at[1]),
         pltpu.make_async_copy(gain_h.at[pl.ds(pl.multiple_of(t * 16, 16), 16)], gain_v, load_sem.at[2]),
         pltpu.make_async_copy(master_h, ma_v, load_sem.at[3]),
@@ -93,8 +93,16 @@
         pltpu.make_async_copy(query_h, q_v, load_sem.at[6]),
         pltpu.make_async_copy(fresh_h, f_v, load_sem.at[7]),
         pltpu.make_async_copy(cache_h, kv_v, load_sem.at[8]),
+        pltpu.make_async_copy(length_h, length_ref, load_sem.at[9]),
+        pltpu.make_async_copy(table_h, table_ref, load_sem.at[10]),
     ]
-    loads[0].start()
+    quarters = [
+        pltpu.make_async_copy(
+            grad_h.at[k // 2, pl.ds(k % 2 * 32, 32)], g_v.at[k // 2, pl.ds(k % 2 * 32, 32)], quarter_sem.at[k])
+        for k in range(4)
+    ]
+    for quarter in quarters:
+        quarter.start()
     loads[1].start()
     barrier = pltpu.get_barrier_semaphore()
     greeted = near + far + [team[k] for k in (2, 3, 4, 6)]
@@ -108,19 +116,20 @@
         used.append(r)
         return r
 
-    loads[0].wait()
-    for load in loads[2:]:
-        load.start()
-
-    def square(i, acc):
-        g = g_v[i // 4, pl.ds(pl.multiple_of((i % 4) * 16, 16), 16), :].astype(F32)
-        gf[i // 4, pl.ds(pl.multiple_of((i % 4) * 16, 16), 16), :] = g
-        sq = g * g
-        return acc + (sq[:8] + sq[8:])
-
-    acc = lax.fori_loop(0, 8, square, jnp.zeros((8, K_DEV), F32))
+    acc = jnp.zeros((8, K_DEV), F32)
+    for k in range(4):
+        quarters[k].wait()
+        if k == 0:
+            for load in loads[2:]:
+                load.start()
+        for r in range(2):
+            rows = pl.ds(k % 2 * 32 + r * 16, 16)
+            g = g_v[k // 2, rows, :].astype(F32)
+            gf[k // 2, rows, :] = g
+            sq = g * g
+            acc += sq[:8] + sq[8:]
     local = jnp.sum(jnp.sum(acc, axis=0, keepdims=True), axis=1, keepdims=True)
-    p_s[0] = jnp.broadcast_to(local, (8, 128))
+    p_s[0] = jnp.broadcast_to(local, (1, 128))
 
     pl.semaphore_wait(barrier, len(greeted))
 
@@ -149,15 +158,6 @@
     rows_x = [remote(rows_of(0, c, r), rows_of(1, c, r), to_xp) for r in range(2)]
     rows_y = [remote(rows_of(0, c, r), rows_of(2, c, r), to_yp) for r in range(2)]
     core_rows = [to_other_core(0, 0), to_other_core(0, 1)]
-
-    own_len = jnp.where(
-        lax.broadcasted_iota(jnp.int32, (32, ROWS), 1) // 8
-        == lax.broadcasted_iota(jnp.int32, (32, ROWS), 0),
-        jnp.broadcast_to(length_ref[...].astype(F32), (32, ROWS)), 0.0).astype(BF16)
-    spread_len = jnp.where(
-        lax.broadcasted_iota(jnp.int32, (ROWS, 128), 0) % 8
-        == lax.broadcasted_iota(jnp.int32, (ROWS, 128), 1) // 16, 1.0, 0.0).astype(BF16)
-    len_v[...] = jnp.dot(own_len, spread_len, preferred_element_type=F32)
 
     def attend_block(g):
         rows = pl.ds(pl.multiple_of(g * 8, 8), 8)
@@ -213,11 +213,19 @@
         for part in (high, low):
             row_squares += lax.dot_general(ones, part, (((1,), (1,)), ((), ())), preferred_element_type=F32)
 
-    t_s[...] = row_squares
+    t_s[...] = row_squares[0:1, :]
     to_all(t_s, t_r, team, 4)
 
     for load in loads[6:]:
         load.wait()
+    own_len = jnp.where(
+        lax.broadcasted_iota(jnp.int32, (32, ROWS), 1) // 8
+        == lax.broadcasted_iota(jnp.int32, (32, ROWS), 0),
+        jnp.broadcast_to(length_ref[...].astype(F32), (32, ROWS)), 0.0).astype(BF16)
+    spread_len = jnp.where(
+        lax.broadcasted_iota(jnp.int32, (ROWS, 128), 0) % 8
+        == lax.broadcasted_iota(jnp.int32, (ROWS, 128), 1) // 16, 1.0, 0.0).astype(BF16)
+    len_v[...] = jnp.dot(own_len, spread_len, preferred_element_type=F32)
     attend(0, 8)
 
     from_all(p_r.at[1], 2)
@@ -247,12 +255,6 @@
 
     @pl.loop(0, 4)
     def _(zone):
-        b_swap[pl.ds(pl.multiple_of(zone * 16, 16), 16), :] = fresh(oc, zone)
-
-    swap = remote(b_swap, b_v.at[0, c], to_core, b_v.at[0, oc])
-
-    @pl.loop(0, 4)
-    def _(zone):
         b_v[0, c, pl.ds(pl.multiple_of(zone * 16, 16), 16), :] = fresh(c, zone)
 
     def units(src, dst, k, device):
@@ -260,12 +262,21 @@
         return remote(b_v.at[src, half], b_v.at[dst, half], device)
 
     unit = {}
-    for k in range(2):
-        if k == 1:
-            swap.came()
+
+    def units_out(k):
         unit[1, k] = units(0, 1, k, to_zl)
         unit[2, k] = units(0, 2, k, to_xq)
         unit[3, k] = units(0, 3, k, to_yq)
+
+    units_out(0)
+
+    @pl.loop(0, 4)
+    def _(zone):
+        b_swap[pl.ds(pl.multiple_of(zone * 16, 16), 16), :] = fresh(oc, zone)
+
+    swap = remote(b_swap, b_v.at[0, c], to_core, b_v.at[0, oc])
+    swap.came()
+    units_out(1)
 
     spread = (lax.broadcasted_iota(jnp.int32, (32, 256), 0)
               == lax.broadcasted_iota(jnp.int32, (32, 256), 1) // 8).astype(F32).astype(BF16)
@@ -318,10 +329,6 @@
     unit[3, 1].came()
     unit[6, 1] = units(3, 6, 1, to_xq)
     unit[2, 1].came()
-    pass_rows(1)
-    for r in core_rows + core_got:
-        r.came()
-
     def half_product(slot, count, a, h):
         lhs = b_v[slot:slot + count, h].reshape(count * UNITS, K_DEV)
         return lax.dot_general(lhs, a_v[a, h], (((1,), (1,)), ((), ())), preferred_element_type=F32)
@@ -343,11 +350,19 @@
             z = (zh + k) % 4
             sums.append(remote(view_s(z), view_r(k - 1), at(x, zl, y, z, c)))
 
-    @pl.loop(0, 3)
+    for r in core_rows:
+        r.came()
+    tile(0, 2, 0)
+    send_sums(lambda z: c_s.at[pl.ds(0, 2), z, 0], lambda k: c_r.at[k, pl.ds(0, 2), 0])
+    pass_rows(1)
+    for r in core_got:
+        r.came()
+
+    @pl.loop(1, 3)
     def _(a):
         tile(0, 2, a)
 
-    send_sums(lambda z: c_s.at[pl.ds(0, 2), z, pl.ds(0, 3)], lambda k: c_r.at[k, pl.ds(0, 2), pl.ds(0, 3)])
+    send_sums(lambda z: c_s.at[pl.ds(0, 2), z, pl.ds(1, 2)], lambda k: c_r.at[k, pl.ds(0, 2), pl.ds(1, 2)])
     unit[4, 0].came()
     unit[7, 0] = units(4, 7, 0, to_yq)
     unit[5, 0].came()
@@ -401,7 +416,7 @@
         r.came()
 
     def activations(a, p):
-        scale = lax.rsqrt(s_g[a][0:1, :] * (1.0 / WIDTH) + NORM_EPSILON)
+        scale = lax.rsqrt(s_g[a] * (1.0 / WIDTH) + NORM_EPSILON)
         v = c_s[p, zh, a].astype(F32)
         for k in range(3):
             v += c_r[k, p, a].astype(F32)
@@ -410,17 +425,19 @@
         hidden = (gate / (1.0 + jnp.exp(-gate)) * up).reshape(16, ROWS).astype(BF16)
         h_s[a, p * 16:(p + 1) * 16, :] = hidden
 
-    for r in sums[:9]:
-        r.came()
-    for a in range(4):
+    for r in sums[:12]:
+        r.came()
+    outs = []
+    for a, device in ((3, to_diag), (1, to_xp), (2, to_yp), (0, None)):
         for p in range(3):
             activations(a, p)
-    for r in sums[9:]:
-        r.came()
-    outs = []
+        if device is not None:
+            outs.append(remote(h_s.at[a, pl.ds(0, 48)], h_r.at[a, pl.ds(0, 48)], device))
+    for r in sums[12:]:
+        r.came()
     for a, device in ((3, to_diag), (1, to_xp), (2, to_yp)):
         activations(a, 3)
-        outs.append(remote(h_s.at[a], h_r.at[a], device))
+        outs.append(remote(h_s.at[a, pl.ds(48, 16)], h_r.at[a, pl.ds(48, 16)], device))
     activations(0, 3)
     h_r[0] = h_s[0]
     for r in outs:
@@ -450,7 +467,7 @@
             pltpu.VMEM(queries.shape, BF16),
             pltpu.VMEM((ROWS, 256), BF16),
         ),
-        in_specs=[hbm] * 9 + [vmem] * 2,
+        in_specs=[hbm] * 11,
         out_specs=(vmem,) * 4,
         scratch_shapes=[
             pltpu.VMEM(slab, BF16),
@@ -466,18 +483,21 @@
             pltpu.VMEM((3, 4, 4, 2, 16, ROWS), BF16),
             pltpu.VMEM((4, UNITS, ROWS), BF16),
             pltpu.VMEM((4, UNITS, ROWS), BF16),
-            pltpu.VMEM((2, 8, 128), F32),
-            pltpu.VMEM((2, 15, 8, 128), F32),
-            pltpu.VMEM((8, ROWS), F32),
-            pltpu.VMEM((7, 8, ROWS), F32),
-            pltpu.VMEM((4, 8, ROWS), F32),
+            pltpu.VMEM((2, 1, 128), F32),
+            pltpu.VMEM((2, 15, 1, 128), F32),
+            pltpu.VMEM((1, ROWS), F32),
+            pltpu.VMEM((7, 1, ROWS), F32),
+            pltpu.VMEM((4, 1, ROWS), F32),
             pltpu.VMEM(queries.shape, BF16),
             pltpu.VMEM((ROWS, 2, 32, 128), BF16),
             pltpu.VMEM((ROWS, 1, 2, 128), BF16),
             pltpu.VMEM((32, 128), F32),
             pltpu.VMEM((4, UNITS, ROWS), F32),
             pltpu.VMEM((256, 256), BF16),
-            pltpu.SemaphoreType.DMA((9,)),
+            pltpu.VMEM((1, ROWS), jnp.int32),
+            pltpu.VMEM((1, 32), jnp.int32),
+            pltpu.SemaphoreType.DMA((11,)),
+            pltpu.SemaphoreType.DMA((4,)),
             pltpu.SemaphoreType.DMA((N_COPIES,)),
             pltpu.SemaphoreType.DMA((N_COPIES,)),
             pltpu.SemaphoreType.DMA((6,)),

time: 74.5 us -> 72.8 us (0.977)
  Pallas kernels: 73.4 us -> 72 us
    pallas_call x1, Pallas kernels: 71.7 us -> 70.3 us  [step(): pl.pallas_call(kernel, out_shape=(pltpu.VMEM(slab, F32), pltpu.VMEM(slab,...]
where the time goes in v5:
time: 72.8 us; the launch traced here: 72.7 us
  Pallas kernels  72 us (99%)
    pallas_call x1, Pallas kernels, step(): pl.pallas_call(kernel, out_shape=(pltpu.VMEM(slab, F32), pltpu.VMEM(slab,...  70.3 us
    pallas_call x1, Pallas kernels, step(): pl.pallas_call(write, out_shape=[jax.ShapeDtypeStruct(r.shape, r.dtype) f...  1.73 us

profile of v5, /device:TPU:1, one launch (start us, length us, event | category | flops | bytes accessed | tf_op | source)
XLA Modules:
  0.0 72.7 jit_solution(13482162438335912717)
XLA Ops:
  0.6 70.3 %step.1 = (f32[2,64,2048]{2,1,0:T(8,128)S(1)}, f32[2,64,2048]{2,1,0:T(8,128)S(1)}, bf16[256,16,128]{2,1,0:T(8,128)(2,1)S(1)}, bf16[256,256]{1,0:T(8,128)(2,1)S(1)}) custom-call(bf16[2,64,2048]{2,1,0:T(8,128)(2,1)} %refs_0_.1, f32[2,64,2048]{2,1,0:T(8,128)} %refs_1_.1, f32[2,64,2048]{2,1,0:T(8,128)} %refs_2_.1, f32[2,64,2048]{2,1,0:T(8,128)} %refs_3_.1, ...), custom_call_target="tpu_custom_call" | custom-call | tf_op jit(solution)/shard_map/step/pallas_call | solution.py:462
  70.9 1.7 %write.1 = (f32[2,64,2048]{2,1,0:T(8,128)}, f32[2,64,2048]{2,1,0:T(8,128)}, bf16[256,16,128]{2,1,0:T(8,128)(2,1)}, bf16[256,256]{1,0:T(8,128)(2,1)}) custom-call(f32[2,64,2048]{2,1,0:T(8,128)S(1)} %get-tuple-element.8.refs_0_, f32[2,64,2048]{2,1,0:T(8,128)S(1)} %get-tuple-element.9.refs_1_, bf16[256,16,128]{2,1,0:T(8,128)(2,1)S(1)} %get-tuple-element.10.refs_2_, ...), custom_call_target="tpu_custom_call" | custom-call | tf_op jit(solution)/shard_map/write/pallas_call | solution.py:519

commit v6 on v5

--- a/solution.py
+++ b/solution.py
@@ -46,7 +46,7 @@
         self.inbound.wait_recv()
 
 
-N_COPIES = 56
+N_COPIES = 60
 
 
 def step_kernel(
@@ -358,8 +358,7 @@
     for r in core_got:
         r.came()
 
-    @pl.loop(1, 3)
-    def _(a):
+    for a in (1, 2):
         tile(0, 2, a)
 
     send_sums(lambda z: c_s.at[pl.ds(0, 2), z, pl.ds(1, 2)], lambda k: c_r.at[k, pl.ds(0, 2), pl.ds(1, 2)])
@@ -370,8 +369,7 @@
     unit[7, 1] = units(5, 7, 1, to_xq)
     unit[4, 1].came()
 
-    @pl.loop(0, 3)
-    def _(a):
+    for a in range(3):
         tile(2, 1, a)
 
     send_sums(lambda z: c_s.at[2, z, pl.ds(0, 3)], lambda k: c_r.at[k, 2, pl.ds(0, 3)])
@@ -388,8 +386,7 @@
     for k in range(2):
         unit[6, k].came()
 
-    @pl.loop(0, 4)
-    def _(a):
+    for a in range(4):
         out = product(6, 1, a)
         for z in range(4):
             c_s[3, z, a, 0] = out[0, z]
@@ -398,19 +395,21 @@
 
     unit[7, 0].came()
 
-    @pl.loop(0, 4)
-    def _(a):
+    for a in range(4):
         last[a] = half_product(7, 1, a, c)
 
     unit[7, 1].came()
 
-    @pl.loop(0, 4)
-    def _(a):
-        out = (last[a] + half_product(7, 1, a, oc)).reshape(4, 16, ROWS).astype(BF16)
-        for z in range(4):
-            c_s[3, z, a, 1] = out[z]
-
-    send_sums(lambda z: c_s.at[3, z, :, 1], lambda k: c_r.at[k, 3, :, 1])
+    def finish_two(first):
+        for a in (first + 1, first):
+            out = (last[a] + half_product(7, 1, a, oc)).reshape(4, 16, ROWS).astype(BF16)
+            for z in range(4):
+                c_s[3, z, a, 1] = out[z]
+        send_sums(
+            lambda z: c_s.at[3, z, pl.ds(first, 2), 1], lambda k: c_r.at[k, 3, pl.ds(first, 2), 1])
+
+    finish_two(2)
+    finish_two(0)
 
     for r in square_copies:
         r.came()
@@ -433,12 +432,19 @@
             activations(a, p)
         if device is not None:
             outs.append(remote(h_s.at[a, pl.ds(0, 48)], h_r.at[a, pl.ds(0, 48)], device))
-    for r in sums[12:]:
-        r.came()
-    for a, device in ((3, to_diag), (1, to_xp), (2, to_yp)):
+    def last_part(a, device):
         activations(a, 3)
-        outs.append(remote(h_s.at[a, pl.ds(48, 16)], h_r.at[a, pl.ds(48, 16)], device))
-    activations(0, 3)
+        if device is not None:
+            outs.append(remote(h_s.at[a, pl.ds(48, 16)], h_r.at[a, pl.ds(48, 16)], device))
+
+    for r in sums[12:18]:
+        r.came()
+    last_part(3, to_diag)
+    last_part(2, to_yp)
+    for r in sums[18:]:
+        r.came()
+    last_part(1, to_xp)
+    last_part(0, None)
     h_r[0] = h_s[0]
     for r in outs:
         r.came()

time: 72.8 us -> 72.5 us (level)
  no operation moved by 1% of the time
where the time goes in v6:
time: 72.5 us; the launch traced here: 72.4 us
  Pallas kernels  71.7 us (99%)
    pallas_call x1, Pallas kernels, step(): pl.pallas_call(kernel, out_shape=(pltpu.VMEM(slab, F32), pltpu.VMEM(slab,...  70 us
    pallas_call x1, Pallas kernels, step(): pl.pallas_call(write, out_shape=[jax.ShapeDtypeStruct(r.shape, r.dtype) f...  1.73 us

profile of v6, /device:TPU:1, one launch (start us, length us, event | category | flops | bytes accessed | tf_op | source)
XLA Modules:
  0.0 72.4 jit_solution(9979269302000311795)
XLA Ops:
  0.6 70.0 %step.1 = (f32[2,64,2048]{2,1,0:T(8,128)S(1)}, f32[2,64,2048]{2,1,0:T(8,128)S(1)}, bf16[256,16,128]{2,1,0:T(8,128)(2,1)S(1)}, bf16[256,256]{1,0:T(8,128)(2,1)S(1)}) custom-call(bf16[2,64,2048]{2,1,0:T(8,128)(2,1)} %refs_0_.1, f32[2,64,2048]{2,1,0:T(8,128)} %refs_1_.1, f32[2,64,2048]{2,1,0:T(8,128)} %refs_2_.1, f32[2,64,2048]{2,1,0:T(8,128)} %refs_3_.1, ...), custom_call_target="tpu_custom_call" | custom-call | tf_op jit(solution)/shard_map/step/pallas_call | solution.py:468
  70.7 1.7 %write.1 = (f32[2,64,2048]{2,1,0:T(8,128)}, f32[2,64,2048]{2,1,0:T(8,128)}, bf16[256,16,128]{2,1,0:T(8,128)(2,1)}, bf16[256,256]{1,0:T(8,128)(2,1)}) custom-call(f32[2,64,2048]{2,1,0:T(8,128)S(1)} %get-tuple-element.8.refs_0_, f32[2,64,2048]{2,1,0:T(8,128)S(1)} %get-tuple-element.9.refs_1_, bf16[256,16,128]{2,1,0:T(8,128)(2,1)S(1)} %get-tuple-element.10.refs_2_, ...), custom_call_target="tpu_custom_call" | custom-call | tf_op jit(solution)/shard_map/write/pallas_call | solution.py:525

commit v7 on v6

--- a/solution.py
+++ b/solution.py
@@ -216,17 +216,6 @@
     t_s[...] = row_squares[0:1, :]
     to_all(t_s, t_r, team, 4)
 
-    for load in loads[6:]:
-        load.wait()
-    own_len = jnp.where(
-        lax.broadcasted_iota(jnp.int32, (32, ROWS), 1) // 8
-        == lax.broadcasted_iota(jnp.int32, (32, ROWS), 0),
-        jnp.broadcast_to(length_ref[...].astype(F32), (32, ROWS)), 0.0).astype(BF16)
-    spread_len = jnp.where(
-        lax.broadcasted_iota(jnp.int32, (ROWS, 128), 0) % 8
-        == lax.broadcasted_iota(jnp.int32, (ROWS, 128), 1) // 16, 1.0, 0.0).astype(BF16)
-    len_v[...] = jnp.dot(own_len, spread_len, preferred_element_type=F32)
-    attend(0, 8)
 
     from_all(p_r.at[1], 2)
     total = p_s[1]
@@ -277,6 +266,17 @@
     swap = remote(b_swap, b_v.at[0, c], to_core, b_v.at[0, oc])
     swap.came()
     units_out(1)
+
+    for load in loads[6:]:
+        load.wait()
+    own_len = jnp.where(
+        lax.broadcasted_iota(jnp.int32, (32, ROWS), 1) // 8
+        == lax.broadcasted_iota(jnp.int32, (32, ROWS), 0),
+        jnp.broadcast_to(length_ref[...].astype(F32), (32, ROWS)), 0.0).astype(BF16)
+    spread_len = jnp.where(
+        lax.broadcasted_iota(jnp.int32, (ROWS, 128), 0) % 8
+        == lax.broadcasted_iota(jnp.int32, (ROWS, 128), 1) // 16, 1.0, 0.0).astype(BF16)
+    len_v[...] = jnp.dot(own_len, spread_len, preferred_element_type=F32)
 
     spread = (lax.broadcasted_iota(jnp.int32, (32, 256), 0)
               == lax.broadcasted_iota(jnp.int32, (32, 256), 1) // 8).astype(F32).astype(BF16)
@@ -303,7 +303,7 @@
         squares += t_r[k]
     s_g[0] = squares
     square_copies = [remote(s_g.at[0], s_g.at[slot], device) for slot, device in ((1, to_xp), (2, to_yp), (3, to_diag))]
-    attend(8, 32)
+    attend(0, 32)
 
     core_got = []
     diag = []

time: 72.5 us -> 73.3 us (1.011)
  no operation moved by 1% of the time
where the time goes in v7:
time: 73.3 us; the launch traced here: 72.6 us
  Pallas kernels  71.9 us (98%)
    pallas_call x1, Pallas kernels, step(): pl.pallas_call(kernel, out_shape=(pltpu.VMEM(slab, F32), pltpu.VMEM(slab,...  70.2 us
    pallas_call x1, Pallas kernels, step(): pl.pallas_call(write, out_shape=[jax.ShapeDtypeStruct(r.shape, r.dtype) f...  1.73 us

profile of v7, /device:TPU:1, one launch (start us, length us, event | category | flops | bytes accessed | tf_op | source)
XLA Modules:
  0.0 72.6 jit_solution(13792345850715432688)
XLA Ops:
  0.6 70.2 %step.1 = (f32[2,64,2048]{2,1,0:T(8,128)S(1)}, f32[2,64,2048]{2,1,0:T(8,128)S(1)}, bf16[256,16,128]{2,1,0:T(8,128)(2,1)S(1)}, bf16[256,256]{1,0:T(8,128)(2,1)S(1)}) custom-call(bf16[2,64,2048]{2,1,0:T(8,128)(2,1)} %refs_0_.1, f32[2,64,2048]{2,1,0:T(8,128)} %refs_1_.1, f32[2,64,2048]{2,1,0:T(8,128)} %refs_2_.1, f32[2,64,2048]{2,1,0:T(8,128)} %refs_3_.1, ...), custom_call_target="tpu_custom_call" | custom-call | tf_op jit(solution)/shard_map/step/pallas_call | solution.py:468
  70.9 1.7 %write.1 = (f32[2,64,2048]{2,1,0:T(8,128)}, f32[2,64,2048]{2,1,0:T(8,128)}, bf16[256,16,128]{2,1,0:T(8,128)(2,1)}, bf16[256,256]{1,0:T(8,128)(2,1)}) custom-call(f32[2,64,2048]{2,1,0:T(8,128)S(1)} %get-tuple-element.8.refs_0_, f32[2,64,2048]{2,1,0:T(8,128)S(1)} %get-tuple-element.9.refs_1_, bf16[256,16,128]{2,1,0:T(8,128)(2,1)S(1)} %get-tuple-element.10.refs_2_, ...), custom_call_target="tpu_custom_call" | custom-call | tf_op jit(solution)/shard_map/write/pallas_call | solution.py:525
